TPU v7x, 32 devices: a whole 2x2x4 slice. The times are simulated.
32 devices in a mesh: groups: 2 (over y), tm: 4 (over z), stn: 4 (over x, core).
Axes of the slice: x: 2, y: 2, z: 4, core: 2. Of those that a mesh axis runs over, the one named last changes fastest.
Arguments:
- right_side: float32 [256, 7168], P(('groups', 'tm'), 'stn'), parts along dimension 0, may hold values from -8 to 8
- mask: int32 [16, 7168], P(('groups', 'tm'), 'stn'), parts along dimension 0, may hold values 0 or 1
- coords: int32 [2, 14336], P(None, ('groups', 'stn')), parts along dimension 1, may hold values from 0 to 255
- station_scale: float32 [14336], P(('groups', 'stn')), parts along dimension 0, may hold values from 0.5 to 2
Outputs:
- solution_field: float32 [256, 7168], P(('groups', 'tm'), 'stn'), parts along dimension 0
- residual: float32 [256, 7168], P(('groups', 'tm'), 'stn'), parts along dimension 0
There are 2 independent parts, one for each index of `groups`. A program takes and returns all parts, laid end to end along the dimension named above; each array names one. Nothing has to cross between parts.
All inputs are finite; a program needn't handle non-finite values. No bound on the sum of `mask` on one device may be relied on, other than what follows from the above.
Results may differ from a plain program's by a relative error of at most 0.015.
Values may be sent and summed in bfloat16 or wider, within the bound.
No kernel may reach another device: no remote copies, remote signals or barrier semaphores. Data moves between devices by JAX's collectives and lax.ppermute only.
A program may use at most 64 MiB of HBM per device.

v0:
```python
import functools
import math

import jax
import jax.numpy as jnp
from jax import lax
from jax.experimental import pallas as pl
from jax.experimental.pallas import tpu as pltpu
from jax.sharding import PartitionSpec as P


GRID = 256
kernel_norm = 4.0
noise_level = 0.5
slope = math.sqrt(3.0) * 4.0 / GRID
LANES = 128
VMEM = pl.BlockSpec(memory_space=pltpu.VMEM)
MIB = 1024 * 1024


def call(body, out_shape, args, scratch=(), limit=16):
    outs = jax.tree.map(lambda _: VMEM, out_shape)
    return pl.pallas_call(
        body,
        out_shape=out_shape,
        in_specs=[VMEM] * len(args),
        out_specs=outs,
        scratch_shapes=list(scratch),
        compiler_params=pltpu.CompilerParams(vmem_limit_bytes=limit * MIB),
    )(*args)


def features(coords, rows):
    centred = coords.astype(jnp.float32) - GRID / 2.0
    x, y = centred[0:1], centred[1:2]
    square = x * x + y * y
    high = jnp.floor(square * (1.0 / 256.0)) * 256.0
    low = square - high
    one, zero = jnp.ones_like(x), jnp.zeros_like(x)
    if rows:
        return jnp.concatenate([x, y, high, low, one, one, zero, zero], axis=0)
    return jnp.concatenate([-2.0 * x, -2.0 * y, one, one, high, low, zero, zero], axis=0)


def step_of(extent):
    for step in (448, 256, 128, 64, 32, 16):
        if extent % step == 0:
            return step
    return extent


def tile_body(rows_ref, cols_ref, tile_ref, row_features, col_features):
    row_features[...] = features(rows_ref[...], True).T.astype(jnp.bfloat16)
    col_features[...] = features(cols_ref[...], False).astype(jnp.bfloat16)
    step = step_of(tile_ref.shape[0])

    def body(index, carry):
        at = pl.ds(pl.multiple_of(index * step, step), step)
        square = jnp.dot(
            row_features[at, :], col_features[...], preferred_element_type=jnp.float32
        )
        distance = square * lax.rsqrt(jnp.maximum(square, 1e-20))
        decay = jnp.exp2(distance * (-slope * math.log2(math.e)))
        tile_ref[at, :] = ((1.0 / kernel_norm + slope / kernel_norm * distance) * decay).astype(
            jnp.bfloat16
        )
        return carry

    lax.fori_loop(0, tile_ref.shape[0] // step, body, 0)


def matern_tile(rows, cols):
    extent, width = rows.shape[1], cols.shape[1]
    return call(
        tile_body,
        jax.ShapeDtypeStruct((extent, width), jnp.bfloat16),
        (rows, cols),
        scratch=[pltpu.VMEM((extent, 8), jnp.bfloat16), pltpu.VMEM((8, width), jnp.bfloat16)],
    )


def observed_rows(mask_ref, hours):
    block = hours // mask_ref.shape[0]
    width = mask_ref.shape[1]
    mask = mask_ref[...].astype(jnp.float32)
    return jnp.concatenate(
        [jnp.broadcast_to(mask[b : b + 1], (block, width)) for b in range(mask_ref.shape[0])],
        axis=0,
    )


def mask_body(field_ref, mask_ref, scale_ref, out_ref):
    gain = observed_rows(mask_ref, field_ref.shape[0]) * scale_ref[...]
    out_ref[...] = (gain * field_ref[...]).astype(out_ref.dtype)


def smooth_body(low_ref, own_ref, high_ref, out_ref):
    hours = own_ref.shape[0]
    rows = lax.broadcasted_iota(jnp.int32, (hours, 3 * hours), 0)
    cols = lax.broadcasted_iota(jnp.int32, (hours, 3 * hours), 1)
    lag = jnp.abs((rows + hours - cols).astype(jnp.float32))
    frac = lag / (hours + 1.0)
    inner = jnp.maximum(1.0 - frac, 0.0)
    squared = inner * inner
    weight = squared * squared * (4.0 * frac + 1.0) / hours
    weight = jnp.where(lag <= hours, weight, 0.0)
    top = weight.astype(jnp.bfloat16)
    rest = (weight - top.astype(jnp.float32)).astype(jnp.bfloat16)
    field = jnp.concatenate([low_ref[...], own_ref[...], high_ref[...]], axis=0)
    both = jnp.dot(
        jnp.concatenate([top, rest], axis=0), field, preferred_element_type=jnp.float32
    )
    out_ref[...] = (both[:hours] + both[hours:]).astype(out_ref.dtype)


def smoothed(field):
    count = lax.axis_size("tm")
    up = [(i, i + 1) for i in range(count - 1)]
    down = [(i + 1, i) for i in range(count - 1)]
    low = lax.ppermute(field, "tm", up)
    high = lax.ppermute(field, "tm", down)
    return call(smooth_body, jax.ShapeDtypeStruct(field.shape, field.dtype), (low, field, high))


def spread_of(blocks, tiles):
    total = jnp.dot(blocks[0], tiles[0][...], preferred_element_type=jnp.float32)
    for block, tile in zip(blocks[1:], tiles[1:]):
        total += jnp.dot(block, tile[...], preferred_element_type=jnp.float32)
    return total


def first_body(count, *refs):
    blocks, tiles = refs[:count], refs[count : 2 * count]
    field_ref, mask_ref, scale_ref, image_ref, masked_ref = refs[2 * count :]
    spread = spread_of([block[...] for block in blocks], tiles)
    gain = observed_rows(mask_ref, field_ref.shape[0]) * scale_ref[...]
    image = gain * spread + noise_level * field_ref[...]
    image_ref[...] = image
    masked_ref[...] = (gain * image).astype(masked_ref.dtype)


def total(value):
    return jnp.sum(jnp.sum(value, axis=0, keepdims=True), axis=1, keepdims=True)


def second_body(count, gathered_ref, *refs):
    me = lax.axis_index("stn")
    tiles = refs[:count]
    field_ref, image_ref, mask_ref, scale_ref, second_ref, sums_ref = refs[count:]
    spread = spread_of([gathered_ref[lax.rem(me + k, count)] for k in range(count)], tiles)
    gain = observed_rows(mask_ref, field_ref.shape[0]) * scale_ref[...]
    field, image = field_ref[...], image_ref[...]
    second = gain * spread + noise_level * image
    second_ref[...] = second
    norm, product = total(field * field), total(field * image)
    guess = norm / jnp.maximum(jnp.maximum(product, noise_level * norm), 1e-30)
    near = field - guess * image
    near_image = image - guess * second
    values = (
        norm,
        product,
        guess,
        total(near * near),
        total(near * image),
        total(image * image),
        total(near * near_image),
        total(near * second + image * near_image),
        total(image * second),
    )
    lane = lax.broadcasted_iota(jnp.int32, sums_ref.shape, 1)
    row = jnp.zeros(sums_ref.shape, jnp.float32)
    for index, value in enumerate(values):
        row = jnp.where(lane == index, value, row)
    sums_ref[...] = row


def last_body(sums_ref, field_ref, image_ref, second_ref, solution_ref, residual_ref):
    sums = sums_ref[...]
    norm, product, guess, near2, near_image, image2, cross0, cross1, cross2 = (
        sums[:, k : k + 1] for k in range(9)
    )
    norm_now, product_now = total(norm), total(product)
    alpha = norm_now / product_now
    off = alpha - guess
    norm_next = total(near2 - 2.0 * off * near_image + off * off * image2)
    product_next = total(cross0 - off * cross1 + off * off * cross2)
    ratio = norm_next / norm_now
    alpha_next = norm_next / (product_next - ratio * norm_next / alpha)
    field, image = field_ref[...], image_ref[...]
    residual = field - alpha * image
    along = (image - alpha * second_ref[...]) + ratio * image
    direction = residual + ratio * field
    solution_ref[...] = alpha * field + alpha_next * direction
    residual_ref[...] = residual - alpha_next * along


def local(right_side, mask, coords, station_scale):
    count = lax.axis_size("stn")
    everyone = count * lax.axis_size("tm")
    hours, width = right_side.shape
    scale = station_scale[None, :]
    block = jax.ShapeDtypeStruct((hours, width), jnp.bfloat16)
    wide = jax.ShapeDtypeStruct((hours, width), jnp.float32)

    def from_ahead(value, offset):
        if offset == 0:
            return value
        return lax.ppermute(value, "stn", [((i + offset) % count, i) for i in range(count)])

    masked = call(mask_body, block, (right_side, mask, scale))
    tiles = []
    for k in range(count):
        rows = from_ahead(coords, k)
        tiles.append(matern_tile(rows, coords))
    smooth = smoothed(masked)
    blocks = [from_ahead(smooth, k) for k in range(count)]
    image, masked = call(
        functools.partial(first_body, count),
        (wide, block),
        (*blocks, *tiles, right_side, mask, scale),
    )
    gathered = lax.all_gather(smoothed(masked), "stn")
    second, sums = call(
        functools.partial(second_body, count),
        (wide, jax.ShapeDtypeStruct((everyone, LANES), jnp.float32)),
        (gathered, *tiles, right_side, image, mask, scale),
    )
    sums = lax.all_to_all(sums, ("tm", "stn"), 0, 0, tiled=True)
    return call(last_body, (wide, wide), (sums, right_side, image, second))


def solution(mesh):
    placed = (
        P(("groups", "tm"), "stn"),
        P(("groups", "tm"), "stn"),
        P(None, ("groups", "stn")),
        P(("groups", "stn")),
    )
    return jax.shard_map(
        local,
        mesh=mesh,
        in_specs=placed,
        out_specs=(P(("groups", "tm"), "stn"), P(("groups", "tm"), "stn")),
        check_vma=False,
    )
```

profile of v0, /device:TPU:0, one launch (start us, length us, event | category | flops | bytes accessed | tf_op | source)
XLA Modules:
  0.0 80.2 jit_solution(10378024346105008229)
XLA Ops:
  0.6 0.7 broadcast_in_dim.3.scale_ref.refs_10_.refs_7_
  1.3 0.0 copy-start
  1.3 0.9 %copy-done = f32[32,1792]{1,0:T(8,128)S(1)} copy-done((f32[32,1792]{1,0:T(8,128)S(1)}, f32[32,1792]{1,0:T(8,128)}, u32[]{:S(2)}) %copy-start) | copy-done | bytes 229400
  2.3 0.0 copy-start.3
  2.3 0.7 copy-done.3
  3.0 1.3 %collective-permute-start.1 = (bf16[32,1792]{1,0:T(8,128)(2,1)S(1)}, bf16[32,1792]{1,0:T(8,128)(2,1)S(1)}, u32[]{:S(2)}, u32[]{:S(2)}) collective-permute-start(bf16[32,1792]{1,0:T(8,128)(2,1)S(1)} %shard_map.59.own_ref), channel_id=1, source_target_pairs={{4,0},{8,4},{12,8},{5,1},{9,5},{13,9},{6,2},{10,6},{14,10},{7,3},{... | collective-permute-start | bytes 344072 | tf_op jit(solution)/shard_map/ppermute | solution.py:121
  4.3 5.6 %collective-permute-start = (bf16[32,1792]{1,0:T(8,128)(2,1)S(1)}, bf16[32,1792]{1,0:T(8,128)(2,1)S(1)}, u32[]{:S(2)}, u32[]{:S(2)}) collective-permute-start(bf16[32,1792]{1,0:T(8,128)(2,1)S(1)} %shard_map.59.own_ref), channel_id=1, source_target_pairs={{0,4},{4,8},{8,12},{1,5},{5,9},{9,13},{2,6},{6,10},{10,14},{3,7},{... | collective-permute-start | bytes 344072 | tf_op jit(solution)/shard_map/ppermute | solution.py:120
  9.9 1.2 %collective-permute-done.1.high_ref = bf16[32,1792]{1,0:T(8,128)(2,1)S(1)} collective-permute-done((bf16[32,1792]{1,0:T(8,128)(2,1)S(1)}, bf16[32,1792]{1,0:T(8,128)(2,1)S(1)}, u32[]{:S(2)}, u32[]{:S(2)}) %collective-permute-start.1) | collective-permute-done | bytes 114720 | tf_op jit(solution)/shard_map/ppermute | solution.py:121
  11.1 1.2 %collective-permute-done.low_ref = bf16[32,1792]{1,0:T(8,128)(2,1)S(1)} collective-permute-done((bf16[32,1792]{1,0:T(8,128)(2,1)S(1)}, bf16[32,1792]{1,0:T(8,128)(2,1)S(1)}, u32[]{:S(2)}, u32[]{:S(2)}) %collective-permute-start) | collective-permute-done | bytes 114720 | tf_op jit(solution)/shard_map/ppermute | solution.py:120
  12.3 0.2 shard_map.60.refs_0_
  12.5 0.1 collective-permute-start.4
  12.6 2.0 %collective-permute-start.3 = (bf16[32,1792]{1,0:T(8,128)(2,1)S(1)}, bf16[32,1792]{1,0:T(8,128)(2,1)S(1)}, u32[]{:S(2)}, u32[]{:S(2)}) collective-permute-start(bf16[32,1792]{1,0:T(8,128)(2,1)S(1)} %shard_map.60.refs_0_), channel_id=1, source_target_pairs={{2,0},{3,1},{0,2},{1,3},{6,4},{7,5},{4,6},{5,7},{10,8},{11,9},{8,1... | collective-permute-start | bytes 344072 | tf_op jit(solution)/shard_map/ppermute | solution.py:208
  14.5 1.4 %collective-permute-start.2 = (bf16[32,1792]{1,0:T(8,128)(2,1)S(1)}, bf16[32,1792]{1,0:T(8,128)(2,1)S(1)}, u32[]{:S(2)}, u32[]{:S(2)}) collective-permute-start(bf16[32,1792]{1,0:T(8,128)(2,1)S(1)} %shard_map.60.refs_0_), channel_id=1, source_target_pairs={{1,0},{2,1},{3,2},{0,3},{5,4},{6,5},{7,6},{4,7},{9,8},{10,9},{11,1... | collective-permute-start | bytes 344072 | tf_op jit(solution)/shard_map/ppermute | solution.py:208
  15.9 0.0 collective-permute-start.7
  15.9 1.7 %collective-permute-start.5 = (s32[2,1792]{1,0:T(2,128)}, s32[2,1792]{1,0:T(2,128)S(1)}, u32[]{:S(2)}, u32[]{:S(2)}) collective-permute-start(s32[2,1792]{1,0:T(2,128)} %cols_ref.7), channel_id=1, source_target_pairs={{1,0},{2,1},{3,2},{0,3},{5,4},{6,5},{7,6},{4,7},{9,8},{10,9},{11,1... | collective-permute-start | bytes 43016 | tf_op jit(solution)/shard_map/ppermute | solution.py:208
  17.7 2.4 %collective-permute-done.7.rows_ref = s32[2,1792]{1,0:T(2,128)S(1)} collective-permute-done((s32[2,1792]{1,0:T(2,128)}, s32[2,1792]{1,0:T(2,128)S(1)}, u32[]{:S(2)}, u32[]{:S(2)}) %collective-permute-start.7) | collective-permute-done | bytes 14368 | tf_op jit(solution)/shard_map/ppermute | solution.py:208
  20.1 1.9 %collective-permute-start.6 = (s32[2,1792]{1,0:T(2,128)}, s32[2,1792]{1,0:T(2,128)S(1)}, u32[]{:S(2)}, u32[]{:S(2)}) collective-permute-start(s32[2,1792]{1,0:T(2,128)} %cols_ref.7), channel_id=1, source_target_pairs={{2,0},{3,1},{0,2},{1,3},{6,4},{7,5},{4,6},{5,7},{10,8},{11,9},{8,1... | collective-permute-start | bytes 43016 | tf_op jit(solution)/shard_map/ppermute | solution.py:208
  22.0 0.0 copy-start.2
  22.0 0.7 copy-done.2
  22.7 4.7 %shard_map.61.refs_4_.refs_0_ = bf16[1792,1792]{1,0:T(8,128)(2,1)S(1)} custom-call(s32[2,1792]{1,0:T(2,128)S(1)} %copy-done.2, s32[2,1792]{1,0:T(2,128)S(1)} %copy-done.2), custom_call_target="tpu_custom_call" | custom-call | tf_op jit(solution)/shard_map/pallas_call | solution.py:23
  27.4 4.7 %shard_map.64.refs_7_.refs_3_ = bf16[1792,1792]{1,0:T(8,128)(2,1)S(1)} custom-call(s32[2,1792]{1,0:T(2,128)S(1)} %collective-permute-done.7.rows_ref, s32[2,1792]{1,0:T(2,128)S(1)} %copy-done.2), custom_call_target="tpu_custom_call" | custom-call | tf_op jit(solution)/shard_map/pallas_call | solution.py:23
  32.1 0.0 copy-start.1
  32.1 0.0 copy-start.4
  32.1 0.0 collective-permute-done.5.rows_ref
  32.1 4.7 %shard_map.62.refs_5_.refs_1_ = bf16[1792,1792]{1,0:T(8,128)(2,1)S(1)} custom-call(s32[2,1792]{1,0:T(2,128)S(1)} %collective-permute-done.5.rows_ref, s32[2,1792]{1,0:T(2,128)S(1)} %copy-done.2), custom_call_target="tpu_custom_call" | custom-call | tf_op jit(solution)/shard_map/pallas_call | solution.py:23
  36.8 0.0 collective-permute-done.6.rows_ref
  36.8 4.7 %shard_map.63.refs_6_.refs_2_ = bf16[1792,1792]{1,0:T(8,128)(2,1)S(1)} custom-call(s32[2,1792]{1,0:T(2,128)S(1)} %collective-permute-done.6.rows_ref, s32[2,1792]{1,0:T(2,128)S(1)} %copy-done.2), custom_call_target="tpu_custom_call" | custom-call | tf_op jit(solution)/shard_map/pallas_call | solution.py:23
  41.5 0.0 collective-permute-done.4.refs_3_
  41.5 0.0 collective-permute-done.3.refs_2_
  41.6 0.0 collective-permute-done.2.refs_1_
  41.6 0.0 copy-done.1
  41.6 0.0 copy-done.4
  41.6 4.5 %shard_map.65 = (f32[32,1792]{1,0:T(8,128)S(1)}, bf16[32,1792]{1,0:T(8,128)(2,1)S(1)}) custom-call(bf16[32,1792]{1,0:T(8,128)(2,1)S(1)} %shard_map.60.refs_0_, bf16[32,1792]{1,0:T(8,128)(2,1)S(1)} %collective-permute-done.2.refs_1_, bf16[32,1792]{1,0:T(8,128)(2,1)S(1)} %collective-permute-done.3.refs_2_, ...), custom_call_target="tpu_custom_call" | custom-call | tf_op jit(solution)/shard_map/pallas_call | solution.py:23
  46.1 1.3 %collective-permute-start.9 = (bf16[32,1792]{1,0:T(8,128)(2,1)S(1)}, bf16[32,1792]{1,0:T(8,128)(2,1)S(1)}, u32[]{:S(2)}, u32[]{:S(2)}) collective-permute-start(bf16[32,1792]{1,0:T(8,128)(2,1)S(1)} %get-tuple-element.6.own_ref), channel_id=1, source_target_pairs={{4,0},{8,4},{12,8},{5,1},{9,5},{13,9},{6,2},{10,6},{14,10},{7,3},{... | collective-permute-start | bytes 344072 | tf_op jit(solution)/shard_map/ppermute | solution.py:121
  47.4 5.0 %collective-permute-start.8 = (bf16[32,1792]{1,0:T(8,128)(2,1)S(1)}, bf16[32,1792]{1,0:T(8,128)(2,1)S(1)}, u32[]{:S(2)}, u32[]{:S(2)}) collective-permute-start(bf16[32,1792]{1,0:T(8,128)(2,1)S(1)} %get-tuple-element.6.own_ref), channel_id=1, source_target_pairs={{0,4},{4,8},{8,12},{1,5},{5,9},{9,13},{2,6},{6,10},{10,14},{3,7},{... | collective-permute-start | bytes 344072 | tf_op jit(solution)/shard_map/ppermute | solution.py:120
  52.4 0.8 %collective-permute-done.9.high_ref = bf16[32,1792]{1,0:T(8,128)(2,1)S(1)} collective-permute-done((bf16[32,1792]{1,0:T(8,128)(2,1)S(1)}, bf16[32,1792]{1,0:T(8,128)(2,1)S(1)}, u32[]{:S(2)}, u32[]{:S(2)}) %collective-permute-start.9) | collective-permute-done | bytes 114720 | tf_op jit(solution)/shard_map/ppermute | solution.py:121
  53.2 1.5 %collective-permute-done.8.low_ref = bf16[32,1792]{1,0:T(8,128)(2,1)S(1)} collective-permute-done((bf16[32,1792]{1,0:T(8,128)(2,1)S(1)}, bf16[32,1792]{1,0:T(8,128)(2,1)S(1)}, u32[]{:S(2)}, u32[]{:S(2)}) %collective-permute-start.8) | collective-permute-done | bytes 114720 | tf_op jit(solution)/shard_map/ppermute | solution.py:120
  54.7 0.2 shard_map.66
  54.9 6.5 %all-gather = bf16[128,1792]{1,0:T(8,128)(2,1)S(1)} all-gather(bf16[32,1792]{1,0:T(8,128)(2,1)S(1)} %shard_map.66), channel_id=2, replica_groups=mesh['groups'=2,'tm'=4,'stn'=4] {'stn'}, dimensions={0}, use_global_device_ids=true | all-gather | bytes 573440 | tf_op jit(solution)/shard_map/all_gather | solution.py:222
  61.4 4.6 %shard_map.67 = (f32[32,1792]{1,0:T(8,128)S(1)}, f32[16,128]{1,0:T(8,128)S(1)}) custom-call(bf16[4,32,1792]{2,1,0:T(8,128)(2,1)S(1)} %bitcast.5, bf16[1792,1792]{1,0:T(8,128)(2,1)S(1)} %shard_map.61.refs_4_.refs_0_, bf16[1792,1792]{1,0:T(8,128)(2,1)S(1)} %shard_map.62.refs_5_.refs_1_, bf16[1792,1792]{1,0:T(8,128)(2,1)S(1)} %shard_map.63.refs_6_.refs_2_, ...), custom_call_target="tpu_custom_call" | custom-call | tf_op jit(solution)/shard_map/pallas_call | solution.py:23
  66.1 12.9 %all_to_all.11 = f32[16,1,128]{2,1,0:T(1,128)S(1)} all-to-all(f32[16,1,128]{2,1,0:T(1,128)S(1)} %bitcast.7), channel_id=1, replica_groups=mesh['groups'=2,'tm'=4,'stn'=4] {'tm','stn'}, dimensions={0} | all-to-all | bytes 16384 | tf_op jit(solution)/shard_map/all_to_all | solution.py:228
  79.0 1.2 %shard_map.68 = (f32[32,1792]{1,0:T(8,128)}, f32[32,1792]{1,0:T(8,128)}) custom-call(f32[16,128]{1,0:T(8,128)S(1)} %bitcast.6, f32[32,1792]{1,0:T(8,128)S(1)} %copy-done.1, f32[32,1792]{1,0:T(8,128)S(1)} %get-tuple-element.7.refs_5_.image_ref, f32[32,1792]{1,0:T(8,128)S(1)} %get-tuple-element.9.second_ref), custom_call_target="tpu_custom_call" | custom-call | tf_op jit(solution)/shard_map/pallas_call | solution.py:23
  (1 shorter events, 0.0 us)
Async XLA Ops:
  1.3 0.9 %copy-start = (f32[32,1792]{1,0:T(8,128)S(1)}, f32[32,1792]{1,0:T(8,128)}, u32[]{:S(2)}) copy-start(f32[32,1792]{1,0:T(8,128)} %field_ref.3) | copy-start | bytes 688132
  2.3 0.7 copy-start.3
  3.0 8.1 %collective-permute-start.1 = (bf16[32,1792]{1,0:T(8,128)(2,1)S(1)}, bf16[32,1792]{1,0:T(8,128)(2,1)S(1)}, u32[]{:S(2)}, u32[]{:S(2)}) collective-permute-start(bf16[32,1792]{1,0:T(8,128)(2,1)S(1)} %shard_map.59.own_ref), channel_id=1, source_target_pairs={{4,0},{8,4},{12,8},{5,1},{9,5},{13,9},{6,2},{10,6},{14,10},{7,3},{... | collective-permute-start | bytes 344072 | tf_op jit(solution)/shard_map/ppermute | solution.py:121
  4.3 8.0 %collective-permute-start = (bf16[32,1792]{1,0:T(8,128)(2,1)S(1)}, bf16[32,1792]{1,0:T(8,128)(2,1)S(1)}, u32[]{:S(2)}, u32[]{:S(2)}) collective-permute-start(bf16[32,1792]{1,0:T(8,128)(2,1)S(1)} %shard_map.59.own_ref), channel_id=1, source_target_pairs={{0,4},{4,8},{8,12},{1,5},{5,9},{9,13},{2,6},{6,10},{10,14},{3,7},{... | collective-permute-start | bytes 344072 | tf_op jit(solution)/shard_map/ppermute | solution.py:120
  12.5 29.0 %collective-permute-start.4 = (bf16[32,1792]{1,0:T(8,128)(2,1)S(1)}, bf16[32,1792]{1,0:T(8,128)(2,1)S(1)}, u32[]{:S(2)}, u32[]{:S(2)}) collective-permute-start(bf16[32,1792]{1,0:T(8,128)(2,1)S(1)} %shard_map.60.refs_0_), channel_id=1, source_target_pairs={{3,0},{0,1},{1,2},{2,3},{7,4},{4,5},{5,6},{6,7},{11,8},{8,9},{9,10... | collective-permute-start | bytes 344072 | tf_op jit(solution)/shard_map/ppermute | solution.py:208
  12.6 29.0 %collective-permute-start.3 = (bf16[32,1792]{1,0:T(8,128)(2,1)S(1)}, bf16[32,1792]{1,0:T(8,128)(2,1)S(1)}, u32[]{:S(2)}, u32[]{:S(2)}) collective-permute-start(bf16[32,1792]{1,0:T(8,128)(2,1)S(1)} %shard_map.60.refs_0_), channel_id=1, source_target_pairs={{2,0},{3,1},{0,2},{1,3},{6,4},{7,5},{4,6},{5,7},{10,8},{11,9},{8,1... | collective-permute-start | bytes 344072 | tf_op jit(solution)/shard_map/ppermute | solution.py:208
  14.5 27.0 %collective-permute-start.2 = (bf16[32,1792]{1,0:T(8,128)(2,1)S(1)}, bf16[32,1792]{1,0:T(8,128)(2,1)S(1)}, u32[]{:S(2)}, u32[]{:S(2)}) collective-permute-start(bf16[32,1792]{1,0:T(8,128)(2,1)S(1)} %shard_map.60.refs_0_), channel_id=1, source_target_pairs={{1,0},{2,1},{3,2},{0,3},{5,4},{6,5},{7,6},{4,7},{9,8},{10,9},{11,1... | collective-permute-start | bytes 344072 | tf_op jit(solution)/shard_map/ppermute | solution.py:208
  15.9 4.2 %collective-permute-start.7 = (s32[2,1792]{1,0:T(2,128)}, s32[2,1792]{1,0:T(2,128)S(1)}, u32[]{:S(2)}, u32[]{:S(2)}) collective-permute-start(s32[2,1792]{1,0:T(2,128)} %cols_ref.7), channel_id=1, source_target_pairs={{3,0},{0,1},{1,2},{2,3},{7,4},{4,5},{5,6},{6,7},{11,8},{8,9},{9,10... | collective-permute-start | bytes 43016 | tf_op jit(solution)/shard_map/ppermute | solution.py:208
  15.9 16.2 %collective-permute-start.5 = (s32[2,1792]{1,0:T(2,128)}, s32[2,1792]{1,0:T(2,128)S(1)}, u32[]{:S(2)}, u32[]{:S(2)}) collective-permute-start(s32[2,1792]{1,0:T(2,128)} %cols_ref.7), channel_id=1, source_target_pairs={{1,0},{2,1},{3,2},{0,3},{5,4},{6,5},{7,6},{4,7},{9,8},{10,9},{11,1... | collective-permute-start | bytes 43016 | tf_op jit(solution)/shard_map/ppermute | solution.py:208
  20.1 16.7 %collective-permute-start.6 = (s32[2,1792]{1,0:T(2,128)}, s32[2,1792]{1,0:T(2,128)S(1)}, u32[]{:S(2)}, u32[]{:S(2)}) collective-permute-start(s32[2,1792]{1,0:T(2,128)} %cols_ref.7), channel_id=1, source_target_pairs={{2,0},{3,1},{0,2},{1,3},{6,4},{7,5},{4,6},{5,7},{10,8},{11,9},{8,1... | collective-permute-start | bytes 43016 | tf_op jit(solution)/shard_map/ppermute | solution.py:208
  22.0 0.7 copy-start.2
  32.1 9.5 %copy-start.1 = (f32[32,1792]{1,0:T(8,128)S(1)}, f32[32,1792]{1,0:T(8,128)}, u32[]{:S(2)}) copy-start(f32[32,1792]{1,0:T(8,128)} %field_ref.3) | copy-start | bytes 688132
  32.1 9.5 %copy-start.4 = (s32[2,1792]{1,0:T(2,128)S(1)}, s32[2,1792]{1,0:T(2,128)}, u32[]{:S(2)}) copy-start(s32[2,1792]{1,0:T(2,128)} %refs_6_.1) | copy-start | bytes 43012
  46.1 7.1 %collective-permute-start.9 = (bf16[32,1792]{1,0:T(8,128)(2,1)S(1)}, bf16[32,1792]{1,0:T(8,128)(2,1)S(1)}, u32[]{:S(2)}, u32[]{:S(2)}) collective-permute-start(bf16[32,1792]{1,0:T(8,128)(2,1)S(1)} %get-tuple-element.6.own_ref), channel_id=1, source_target_pairs={{4,0},{8,4},{12,8},{5,1},{9,5},{13,9},{6,2},{10,6},{14,10},{7,3},{... | collective-permute-start | bytes 344072 | tf_op jit(solution)/shard_map/ppermute | solution.py:121
  47.4 7.3 %collective-permute-start.8 = (bf16[32,1792]{1,0:T(8,128)(2,1)S(1)}, bf16[32,1792]{1,0:T(8,128)(2,1)S(1)}, u32[]{:S(2)}, u32[]{:S(2)}) collective-permute-start(bf16[32,1792]{1,0:T(8,128)(2,1)S(1)} %get-tuple-element.6.own_ref), channel_id=1, source_target_pairs={{0,4},{4,8},{8,12},{1,5},{5,9},{9,13},{2,6},{6,10},{10,14},{3,7},{... | collective-permute-start | bytes 344072 | tf_op jit(solution)/shard_map/ppermute | solution.py:120
where the time goes:
time: 80.7 us; the launch traced here: 80.2 us
  Pallas kernels  29.5 us (37%)
  starting transfers between devices  20.2 us (25%)
  blocking collectives  19.4 us (24%)
  waiting for transfers between devices  7.18 us (9%)
  local copies, waits for them, and re-layouts  3.11 us (4%)
  between operations  0.81 us (1%)
    pallas_call x10, Pallas kernels, call(): pl.pallas_call(body, out_shape=out_shape, in_specs=[VMEM] * len(args), ou...  29.5 us
    all_to_all x1, blocking collectives, local(): sums = lax.all_to_all(sums, ('tm', 'stn'), 0, 0, tiled=True)  12.9 us
    ppermute x2, starting transfers between devices, smoothed(): low = lax.ppermute(field, 'tm', up)  10.6 us
    ppermute x6, starting transfers between devices, from_ahead(): lax.ppermute(value, 'stn', [((i + offset) % count, i) for i in range(coun...  7.04 us
    all_gather x1, blocking collectives, local(): gathered = lax.all_gather(smoothed(masked), 'stn')  6.5 us
    ppermute x2, waiting for transfers between devices, smoothed(): low = lax.ppermute(field, 'tm', up)  2.7 us
    ppermute x2, starting transfers between devices, smoothed(): high = lax.ppermute(field, 'tm', down)  2.58 us
    ppermute x6, waiting for transfers between devices, from_ahead(): lax.ppermute(value, 'stn', [((i + offset) % count, i) for i in range(coun...  2.46 us
  transfers between devices with their start and end apart: 10, of which 5 were waited for; matrix products, arithmetic and copies ran while one was open for 0% of the time, Pallas kernels for 23%

commit v1 on v0

v1 whole, which is shorter than its diff:
```python
import functools
import math

import jax
import jax.numpy as jnp
from jax import lax
from jax.experimental import pallas as pl
from jax.experimental.pallas import tpu as pltpu
from jax.sharding import PartitionSpec as P


GRID = 256
kernel_norm = 4.0
noise_level = 0.5
slope = math.sqrt(3.0) * 4.0 / GRID
LANES = 128
MIB = 1024 * 1024
VMEM = pl.BlockSpec(memory_space=pltpu.VMEM)
HBM = pl.BlockSpec(memory_space=pltpu.HBM)


def call(body, out_shape, args, in_specs=None, scratch=()):
    return pl.pallas_call(
        body,
        out_shape=out_shape,
        in_specs=in_specs or [VMEM] * len(args),
        out_specs=jax.tree.map(lambda _: VMEM, out_shape),
        scratch_shapes=list(scratch),
        compiler_params=pltpu.CompilerParams(vmem_limit_bytes=16 * MIB),
    )(*args)


def load_body(field_hbm, mask_hbm, coords_hbm, scale_hbm, field, coords, gain, masked, mask, scale, sems):
    pairs = ((mask_hbm, mask), (scale_hbm, scale), (field_hbm, field), (coords_hbm, coords))
    copies = [
        pltpu.make_async_copy(source, target, sems.at[k])
        for k, (source, target) in enumerate(pairs)
    ]
    for copy in copies:
        copy.start()
    for copy in copies:
        copy.wait()
    hours, width = field.shape
    block = hours // mask.shape[0]
    observed = mask[...].astype(jnp.float32)
    observed = jnp.concatenate(
        [jnp.broadcast_to(observed[b : b + 1], (block, width)) for b in range(mask.shape[0])],
        axis=0,
    )
    gain[...] = observed * scale[...]
    masked[...] = (gain[...] * field[...]).astype(masked.dtype)


def load(right_side, mask, coords, scale):
    return call(
        load_body,
        (
            jax.ShapeDtypeStruct(right_side.shape, right_side.dtype),
            jax.ShapeDtypeStruct(coords.shape, coords.dtype),
            jax.ShapeDtypeStruct(right_side.shape, jnp.float32),
            jax.ShapeDtypeStruct(right_side.shape, jnp.bfloat16),
        ),
        (right_side, mask, coords, scale),
        in_specs=[HBM] * 4,
        scratch=[
            pltpu.VMEM(mask.shape, mask.dtype),
            pltpu.VMEM(scale.shape, scale.dtype),
            pltpu.SemaphoreType.DMA((4,)),
        ],
    )


def features(coords, rows):
    centred = coords.astype(jnp.float32) - GRID / 2.0
    x, y = centred[0:1], centred[1:2]
    square = x * x + y * y
    high = jnp.floor(square * (1.0 / 256.0)) * 256.0
    low = square - high
    one, zero = jnp.ones_like(x), jnp.zeros_like(x)
    if rows:
        return jnp.concatenate([x, y, high, low, one, one, zero, zero], axis=0)
    return jnp.concatenate([-2.0 * x, -2.0 * y, one, one, high, low, zero, zero], axis=0)


def step_of(extent):
    for step in (896, 512, 256, 128, 64, 32, 16):
        if extent % step == 0:
            return step
    return extent


def tile_body(rows_ref, cols_ref, tile_ref, row_features, col_features):
    row_features[...] = features(rows_ref[...], True).T.astype(jnp.bfloat16)
    col_features[...] = features(cols_ref[...], False).astype(jnp.bfloat16)
    step = step_of(tile_ref.shape[0])

    def body(index, carry):
        at = pl.ds(pl.multiple_of(index * step, step), step)
        square = jnp.dot(
            row_features[at, :], col_features[...], preferred_element_type=jnp.float32
        )
        distance = square * lax.rsqrt(jnp.maximum(square, 1e-20))
        decay = jnp.exp2(distance * (-slope * math.log2(math.e)))
        tile_ref[at, :] = ((1.0 / slope + distance) * decay).astype(jnp.bfloat16)
        return carry

    lax.fori_loop(0, tile_ref.shape[0] // step, body, 0)


tile_gain = slope / kernel_norm


def matern_tile(rows, cols):
    extent, width = rows.shape[1], cols.shape[1]
    return call(
        tile_body,
        jax.ShapeDtypeStruct((extent, width), jnp.bfloat16),
        (rows, cols),
        scratch=[pltpu.VMEM((extent, 8), jnp.bfloat16), pltpu.VMEM((8, width), jnp.bfloat16)],
    )


def hour_sum(first, own, second):
    hours = own.shape[0]
    turn = 1 - 2 * lax.rem(lax.axis_index("tm"), 2)
    rows = lax.broadcasted_iota(jnp.int32, (hours, 3 * hours), 0)
    cols = lax.broadcasted_iota(jnp.int32, (hours, 3 * hours), 1)
    part = jnp.where(cols >= hours, 1, 0) + jnp.where(cols >= 2 * hours, 1, 0)
    lag = rows - cols + part * hours - (1 - part) * (turn * hours)
    lag = jnp.abs(lag.astype(jnp.float32))
    frac = lag / (hours + 1.0)
    inner = jnp.maximum(1.0 - frac, 0.0)
    squared = inner * inner
    weight = squared * squared * (4.0 * frac + 1.0) / hours
    weight = jnp.where(lag <= hours, weight, 0.0)
    top = weight.astype(jnp.bfloat16)
    rest = (weight - top.astype(jnp.float32)).astype(jnp.bfloat16)
    both = jnp.dot(
        jnp.concatenate([top, rest], axis=0),
        jnp.concatenate([first, own, second], axis=0),
        preferred_element_type=jnp.float32,
    )
    return both[:hours] + both[hours:]


def smooth_body(first_ref, own_ref, second_ref, out_ref):
    out_ref[...] = hour_sum(first_ref[...], own_ref[...], second_ref[...]).astype(out_ref.dtype)


def halo(field):
    count = lax.axis_size("tm")
    halves = []
    for side in (0, 1):
        pairs = [(i, i + 1) for i in range(side, count - 1, 2)]
        if not pairs:
            halves.append(jnp.zeros_like(field))
            continue
        swaps = pairs + [(b, a) for a, b in pairs]
        halves.append(lax.ppermute(field, "tm", swaps))
    return halves


def from_partner(value, offset):
    count = lax.axis_size("stn")
    if count & (count - 1):
        moves = [((i + offset) % count, i) for i in range(count)]
    else:
        moves = [(i ^ offset, i) for i in range(count)]
    return lax.ppermute(value, "stn", moves)


def gathered(value):
    count = lax.axis_size("stn")
    blocks = {0: value}
    for k in range(1, count):
        low = k & -k
        if count & (count - 1) or low == k:
            blocks[k] = from_partner(value, k)
        else:
            moves = [(i ^ low, i) for i in range(count)]
            blocks[k] = lax.ppermute(blocks[k ^ low], "stn", moves)
    return [blocks[k] for k in range(count)]


def product(blocks, tiles):
    total = jnp.dot(blocks[0][...], tiles[0][...], preferred_element_type=jnp.float32)
    for block, tile in zip(blocks[1:], tiles[1:]):
        total += jnp.dot(block[...], tile[...], preferred_element_type=jnp.float32)
    return total


def first_body(count, *refs):
    blocks, tiles = refs[:count], refs[count : 2 * count]
    field, gain, image, masked = refs[2 * count :]
    spread = tile_gain * product(blocks, tiles)
    image[...] = gain[...] * spread + noise_level * field[...]
    masked[...] = (gain[...] * image[...]).astype(masked.dtype)


def part_body(count, *refs):
    refs[-1][...] = product(refs[:count], refs[count : 2 * count])


def more_body(block, tile, before, out):
    out[...] = before[...] + product([block], [tile])


def sum_all(value):
    return jnp.sum(jnp.sum(value, axis=0, keepdims=True), axis=1, keepdims=True)


def second_body(
    block, tile, before, field_ref, image_ref, a0, m0, b0, a1, m1, b1, spread_ref, sums_ref
):
    spread = tile_gain * (before[...] + product([block], [tile]))
    spread_ref[...] = spread.astype(spread_ref.dtype)
    field, image = field_ref[...], image_ref[...]
    norm, along = sum_all(field * field), sum_all(field * image)
    guess = norm / jnp.maximum(jnp.maximum(along, noise_level * norm), 1e-30)
    near = field - guess * image
    values = (
        norm,
        along,
        guess,
        sum_all(near * near),
        sum_all(near * image),
        sum_all(image * image),
        sum_all(hour_sum(a0[...], m0[...], b0[...]) * spread),
        sum_all(hour_sum(a1[...], m1[...], b1[...]) * spread),
    )
    lane = lax.broadcasted_iota(jnp.int32, sums_ref.shape, 1)
    row = jnp.zeros(sums_ref.shape, jnp.float32)
    for index, value in enumerate(values):
        row = jnp.where(lane == index, value, row)
    sums_ref[...] = row


def last_body(sums_ref, field_ref, image_ref, gain_ref, a, own, b, solution_ref, residual_ref):
    sums = sums_ref[...]
    norm, along, guess, near2, near_image, image2, cross0, cross1 = (
        sums[:, k : k + 1] for k in range(8)
    )
    norm_now = sum_all(norm)
    alpha = norm_now / sum_all(along)
    off = alpha - guess
    norm_next = sum_all(near2 - 2.0 * off * near_image + off * off * image2)
    residual_image = sum_all(near_image - off * image2)
    cross = sum_all(cross0) - alpha * sum_all(cross1)
    product_next = residual_image - alpha * (noise_level * residual_image + cross)
    ratio = norm_next / norm_now
    alpha_next = norm_next / (product_next - ratio * norm_next / alpha)
    field, image = field_ref[...], image_ref[...]
    second = gain_ref[...] * hour_sum(a[...], own[...], b[...]) + noise_level * image
    residual = field - alpha * image
    change = (image - alpha * second) + ratio * image
    direction = residual + ratio * field
    solution_ref[...] = alpha * field + alpha_next * direction
    residual_ref[...] = residual - alpha_next * change


def compute(right_side, mask, coords, station_scale):
    count = lax.axis_size("stn")
    everyone = count * lax.axis_size("tm")
    block = jax.ShapeDtypeStruct(right_side.shape, jnp.bfloat16)
    wide = jax.ShapeDtypeStruct(right_side.shape, jnp.float32)

    field, coords, gain, masked = load(right_side, mask, coords, station_scale[None, :])
    before, after = halo(masked)
    tiles = []
    for rows in gathered(coords):
        tiles.append(matern_tile(rows, coords))
    smooth = call(smooth_body, block, (before, masked, after))
    image, image_masked = call(
        functools.partial(first_body, count),
        (wide, block),
        (*gathered(smooth), *tiles, field, gain),
    )
    blocks = gathered(image_masked)
    image_before, image_after = halo(image_masked)
    ready = min(2, count - 1)
    total = call(functools.partial(part_body, ready), wide, (*blocks[:ready], *tiles[:ready]))
    for k in range(ready, count - 1):
        total = call(more_body, wide, (blocks[k], tiles[k], total))
    spread, sums = call(
        second_body,
        (block, jax.ShapeDtypeStruct((everyone, LANES), jnp.float32)),
        (
            *(blocks[-1], tiles[-1], total, field, image),
            *(before, masked, after),
            *(image_before, image_masked, image_after),
        ),
    )
    last_before, last_after = halo(spread)
    sums = lax.all_to_all(sums, ("tm", "stn"), 0, 0, tiled=True)
    return call(
        last_body, (wide, wide), (sums, field, image, gain, last_before, spread, last_after)
    )


def solution(mesh):
    placed = (
        P(("groups", "tm"), "stn"),
        P(("groups", "tm"), "stn"),
        P(None, ("groups", "stn")),
        P(("groups", "stn")),
    )
    return jax.shard_map(
        compute,
        mesh=mesh,
        in_specs=placed,
        out_specs=(P(("groups", "tm"), "stn"), P(("groups", "tm"), "stn")),
        check_vma=False,
    )
```

time: 80.7 us -> 70.1 us (0.87)
  blocking collectives: 19.4 us -> 11.5 us
  starting transfers between devices: 20.2 us -> 18.7 us
  Pallas kernels: 29.5 us -> 28.2 us
    all_gather x1 -> x0, blocking collectives: 6.5 us -> none  [local(): gathered = lax.all_gather(smoothed(masked), 'stn')]
    ppermute x10 -> x15, starting transfers between devices: 20.2 us -> 18.7 us  [the longest x6 13 us: halo(): halves.append(lax.ppermute(field, 'tm', swaps))]
    all_to_all x1, blocking collectives: 12.9 us -> 11.5 us  [compute(): sums = lax.all_to_all(sums, ('tm', 'stn'), 0, 0, tiled=True)]
    pallas_call x10 -> x11, Pallas kernels: 29.5 us -> 28.2 us  [call(): pl.pallas_call(body, out_shape=out_shape, in_specs=in_specs or [VMEM] * l...]
    ppermute x10 -> x15, waiting for transfers between devices: 7.18 us -> 7.48 us  [the longest x6 4.98 us: from_partner(): return lax.ppermute(value, 'stn', moves)]
    unnamed x10 -> x6, local copies, waits for them, and re-layouts: 2.41 us -> 2.36 us
  transfers between devices with their start and end apart: 10 -> 15, of which waited for: 5 -> 3; matrix products, arithmetic and copies ran while one was open for 0% -> 0% of each run, Pallas kernels for 23% -> 29%
where the time goes in v1:
time: 70.1 us; the launch traced here: 69.7 us
  Pallas kernels  28.2 us (40%)
  starting transfers between devices  18.7 us (27%)
  blocking collectives  11.5 us (16%)
  waiting for transfers between devices  7.48 us (11%)
  local copies, waits for them, and re-layouts  3.06 us (4%)
  between operations  0.79 us (1%)
    pallas_call x11, Pallas kernels, call(): pl.pallas_call(body, out_shape=out_shape, in_specs=in_specs or [VMEM] * l...  28.2 us
    ppermute x6, starting transfers between devices, halo(): halves.append(lax.ppermute(field, 'tm', swaps))  13 us
    all_to_all x1, blocking collectives, compute(): sums = lax.all_to_all(sums, ('tm', 'stn'), 0, 0, tiled=True)  11.5 us
    ppermute x6, starting transfers between devices, from_partner(): return lax.ppermute(value, 'stn', moves)  5.55 us
    ppermute x6, waiting for transfers between devices, from_partner(): return lax.ppermute(value, 'stn', moves)  4.98 us
    ppermute x6, waiting for transfers between devices, halo(): halves.append(lax.ppermute(field, 'tm', swaps))  2.5 us
    unnamed x6, local copies, waits for them, and re-layouts  2.36 us
  transfers between devices with their start and end apart: 15, of which 3 were waited for; matrix products, arithmetic and copies ran while one was open for 0% of the time, Pallas kernels for 29%

profile of v1, /device:TPU:0, one launch (start us, length us, event | category | flops | bytes accessed | tf_op | source)
XLA Modules:
  0.0 69.7 jit_solution(10847906358614362332)
XLA Ops:
  0.6 0.7 %broadcast_in_dim.3.scale_hbm = f32[1,1792]{1,0:T(1,128)S(1)} reshape(f32[1792]{0:T(1024)} %param.7) | data formatting | bytes 14336 | tf_op jit(solution)/shard_map/broadcast_in_dim | solution.py:267
  1.3 0.0 copy-start
  1.3 0.9 %copy-done = f32[32,1792]{1,0:T(8,128)S(1)} copy-done((f32[32,1792]{1,0:T(8,128)S(1)}, f32[32,1792]{1,0:T(8,128)}, u32[]{:S(2)}) %copy-start) | copy-done | bytes 229400
  2.3 0.0 copy-start.1
  2.3 0.7 %copy-done.1 = s32[2,1792]{1,0:T(2,128)S(1)} copy-done((s32[2,1792]{1,0:T(2,128)S(1)}, s32[2,1792]{1,0:T(2,128)}, u32[]{:S(2)}) %copy-start.1) | copy-done | bytes 14360
  3.0 0.0 copy-start.2
  3.0 0.7 %copy-done.2 = s32[2,1792]{1,0:T(2,128)S(1)} copy-done((s32[2,1792]{1,0:T(2,128)S(1)}, s32[2,1792]{1,0:T(2,128)}, u32[]{:S(2)}) %copy-start.2) | copy-done | bytes 14360
  3.7 0.4 shard_map.59
  4.1 3.1 %collective-permute-start = (bf16[32,1792]{1,0:T(8,128)(2,1)S(1)}, bf16[32,1792]{1,0:T(8,128)(2,1)S(1)}, u32[]{:S(2)}, u32[]{:S(2)}) collective-permute-start(bf16[32,1792]{1,0:T(8,128)(2,1)S(1)} %get-tuple-element.10.own_ref.m0), channel_id=1, source_target_pairs={{0,4},{8,12},{4,0},{12,8},{1,5},{9,13},{5,1},{13,9},{2,6},{10,14},... | collective-permute-start | bytes 344072 | tf_op jit(solution)/shard_map/ppermute | solution.py:159
  7.2 0.7 collective-permute-start.1
  7.9 2.5 %collective-permute-done.first_ref.a0 = bf16[32,1792]{1,0:T(8,128)(2,1)S(1)} collective-permute-done((bf16[32,1792]{1,0:T(8,128)(2,1)S(1)}, bf16[32,1792]{1,0:T(8,128)(2,1)S(1)}, u32[]{:S(2)}, u32[]{:S(2)}) %collective-permute-start) | collective-permute-done | bytes 114720 | tf_op jit(solution)/shard_map/ppermute | solution.py:159
  10.4 0.0 collective-permute-done.1.second_ref.b0
  10.4 0.2 shard_map.60.refs_0_
  10.6 1.7 %collective-permute-start.3 = (bf16[32,1792]{1,0:T(8,128)(2,1)S(1)}, bf16[32,1792]{1,0:T(8,128)(2,1)S(1)}, u32[]{:S(2)}, u32[]{:S(2)}) collective-permute-start(bf16[32,1792]{1,0:T(8,128)(2,1)S(1)} %shard_map.60.refs_0_), channel_id=1, source_target_pairs={{2,0},{3,1},{0,2},{1,3},{6,4},{7,5},{4,6},{5,7},{10,8},{11,9},{8,1... | collective-permute-start | bytes 344072 | tf_op jit(solution)/shard_map/ppermute | solution.py:169
  12.3 0.0 collective-permute-start.2
  12.3 3.1 %collective-permute-done.3.refs_2_ = bf16[32,1792]{1,0:T(8,128)(2,1)S(1)} collective-permute-done((bf16[32,1792]{1,0:T(8,128)(2,1)S(1)}, bf16[32,1792]{1,0:T(8,128)(2,1)S(1)}, u32[]{:S(2)}, u32[]{:S(2)}) %collective-permute-start.3) | collective-permute-done | bytes 114720 | tf_op jit(solution)/shard_map/ppermute | solution.py:169
  15.4 0.0 collective-permute-start.4
  15.4 1.7 %collective-permute-start.6 = (s32[2,1792]{1,0:T(2,128)S(1)}, s32[2,1792]{1,0:T(2,128)S(1)}, u32[]{:S(2)}, u32[]{:S(2)}) collective-permute-start(s32[2,1792]{1,0:T(2,128)S(1)} %get-tuple-element.11.rows_ref.cols_ref), channel_id=1, source_target_pairs={{2,0},{3,1},{0,2},{1,3},{6,4},{7,5},{4,6},{5,7},{10,8},{11,9},{8,1... | collective-permute-start | bytes 43016 | tf_op jit(solution)/shard_map/ppermute | solution.py:169
  17.1 0.2 collective-permute-start.5
  17.3 1.8 %collective-permute-done.6.rows_ref = s32[2,1792]{1,0:T(2,128)S(1)} collective-permute-done((s32[2,1792]{1,0:T(2,128)S(1)}, s32[2,1792]{1,0:T(2,128)S(1)}, u32[]{:S(2)}, u32[]{:S(2)}) %collective-permute-start.6) | collective-permute-done | bytes 14368 | tf_op jit(solution)/shard_map/ppermute | solution.py:169
  19.2 0.0 collective-permute-start.7
  19.2 4.2 %shard_map.61.refs_4_.refs_2_ = bf16[1792,1792]{1,0:T(8,128)(2,1)S(1)} custom-call(s32[2,1792]{1,0:T(2,128)S(1)} %get-tuple-element.11.rows_ref.cols_ref, s32[2,1792]{1,0:T(2,128)S(1)} %get-tuple-element.11.rows_ref.cols_ref), custom_call_target="tpu_custom_call" | custom-call | tf_op jit(solution)/shard_map/pallas_call | solution.py:23
  23.4 4.2 %shard_map.63.refs_6_.tile = bf16[1792,1792]{1,0:T(8,128)(2,1)S(1)} custom-call(s32[2,1792]{1,0:T(2,128)S(1)} %collective-permute-done.6.rows_ref, s32[2,1792]{1,0:T(2,128)S(1)} %get-tuple-element.11.rows_ref.cols_ref), custom_call_target="tpu_custom_call" | custom-call | tf_op jit(solution)/shard_map/pallas_call | solution.py:23
  27.6 0.0 collective-permute-done.5.rows_ref
  27.6 4.2 %shard_map.62.refs_5_.refs_3_ = bf16[1792,1792]{1,0:T(8,128)(2,1)S(1)} custom-call(s32[2,1792]{1,0:T(2,128)S(1)} %collective-permute-done.5.rows_ref, s32[2,1792]{1,0:T(2,128)S(1)} %get-tuple-element.11.rows_ref.cols_ref), custom_call_target="tpu_custom_call" | custom-call | tf_op jit(solution)/shard_map/pallas_call | solution.py:23
  31.8 0.0 collective-permute-done.7.rows_ref
  31.8 4.2 %shard_map.64.refs_7_.tile = bf16[1792,1792]{1,0:T(8,128)(2,1)S(1)} custom-call(s32[2,1792]{1,0:T(2,128)S(1)} %collective-permute-done.7.rows_ref, s32[2,1792]{1,0:T(2,128)S(1)} %get-tuple-element.11.rows_ref.cols_ref), custom_call_target="tpu_custom_call" | custom-call | tf_op jit(solution)/shard_map/pallas_call | solution.py:23
  36.0 0.0 collective-permute-done.2.refs_1_
  36.0 0.0 collective-permute-done.4.refs_3_
  36.0 4.5 %shard_map.65 = (f32[32,1792]{1,0:T(8,128)S(1)}, bf16[32,1792]{1,0:T(8,128)(2,1)S(1)}) custom-call(bf16[32,1792]{1,0:T(8,128)(2,1)S(1)} %shard_map.60.refs_0_, bf16[32,1792]{1,0:T(8,128)(2,1)S(1)} %collective-permute-done.2.refs_1_, bf16[32,1792]{1,0:T(8,128)(2,1)S(1)} %collective-permute-done.3.refs_2_, ...), custom_call_target="tpu_custom_call" | custom-call | tf_op jit(solution)/shard_map/pallas_call | solution.py:23
  40.5 1.7 %collective-permute-start.8 = (bf16[32,1792]{1,0:T(8,128)(2,1)S(1)}, bf16[32,1792]{1,0:T(8,128)(2,1)S(1)}, u32[]{:S(2)}, u32[]{:S(2)}) collective-permute-start(bf16[32,1792]{1,0:T(8,128)(2,1)S(1)} %get-tuple-element.14.refs_0_.m1), channel_id=1, source_target_pairs={{2,0},{3,1},{0,2},{1,3},{6,4},{7,5},{4,6},{5,7},{10,8},{11,9},{8,1... | collective-permute-start | bytes 344072 | tf_op jit(solution)/shard_map/ppermute | solution.py:169
  42.2 0.2 collective-permute-start.10
  42.5 4.6 %collective-permute-start.11 = (bf16[32,1792]{1,0:T(8,128)(2,1)S(1)}, bf16[32,1792]{1,0:T(8,128)(2,1)S(1)}, u32[]{:S(2)}, u32[]{:S(2)}) collective-permute-start(bf16[32,1792]{1,0:T(8,128)(2,1)S(1)} %get-tuple-element.14.refs_0_.m1), channel_id=1, source_target_pairs={{0,4},{8,12},{4,0},{12,8},{1,5},{9,13},{5,1},{13,9},{2,6},{10,14},... | collective-permute-start | bytes 344072 | tf_op jit(solution)/shard_map/ppermute | solution.py:159
  47.0 0.8 %collective-permute-start.12 = (bf16[32,1792]{1,0:T(8,128)(2,1)S(1)}, bf16[32,1792]{1,0:T(8,128)(2,1)S(1)}, u32[]{:S(2)}, u32[]{:S(2)}) collective-permute-start(bf16[32,1792]{1,0:T(8,128)(2,1)S(1)} %get-tuple-element.14.refs_0_.m1), channel_id=1, source_target_pairs={{4,8},{8,4},{5,9},{9,5},{6,10},{10,6},{7,11},{11,7},{20,24},{24,20... | collective-permute-start | bytes 344072 | tf_op jit(solution)/shard_map/ppermute | solution.py:159
  47.9 0.0 collective-permute-done.8.block
  47.9 0.1 collective-permute-start.9
  48.0 0.0 collective-permute-done.10.refs_1_
  48.0 2.3 %shard_map.66.before = f32[32,1792]{1,0:T(8,128)S(1)} custom-call(bf16[32,1792]{1,0:T(8,128)(2,1)S(1)} %get-tuple-element.14.refs_0_.m1, bf16[32,1792]{1,0:T(8,128)(2,1)S(1)} %collective-permute-done.10.refs_1_, bf16[1792,1792]{1,0:T(8,128)(2,1)S(1)} %shard_map.61.refs_4_.refs_2_, bf16[1792,1792]{1,0:T(8,128)(2,1)S(1)} %shard_map.62.refs_5_.refs_3_), custom_call_target="tpu_custom_call" | custom-call | tf_op jit(solution)/shard_map/pallas_call | solution.py:23
  50.3 1.2 %shard_map.67.before = f32[32,1792]{1,0:T(8,128)S(1)} custom-call(bf16[32,1792]{1,0:T(8,128)(2,1)S(1)} %collective-permute-done.8.block, bf16[1792,1792]{1,0:T(8,128)(2,1)S(1)} %shard_map.63.refs_6_.tile, f32[32,1792]{1,0:T(8,128)S(1)} %shard_map.66.before), custom_call_target="tpu_custom_call" | custom-call | tf_op jit(solution)/shard_map/pallas_call | solution.py:23
  51.5 0.0 collective-permute-done.11.a1
  51.5 0.0 collective-permute-done.12.b1
  51.5 0.0 collective-permute-done.9.block
  51.5 1.4 %shard_map.68 = (bf16[32,1792]{1,0:T(8,128)(2,1)S(1)}, f32[16,128]{1,0:T(8,128)S(1)}) custom-call(bf16[32,1792]{1,0:T(8,128)(2,1)S(1)} %collective-permute-done.9.block, bf16[1792,1792]{1,0:T(8,128)(2,1)S(1)} %shard_map.64.refs_7_.tile, f32[32,1792]{1,0:T(8,128)S(1)} %shard_map.67.before, f32[32,1792]{1,0:T(8,128)S(1)} %get-tuple-element.12.refs_8_.field_ref, ...), custom_call_target="tpu_custom_call" | custom-call | tf_op jit(solution)/shard_map/pallas_call | solution.py:23
  53.0 3.2 %collective-permute-start.13 = (bf16[32,1792]{1,0:T(8,128)(2,1)S(1)}, bf16[32,1792]{1,0:T(8,128)(2,1)S(1)}, u32[]{:S(2)}, u32[]{:S(2)}) collective-permute-start(bf16[32,1792]{1,0:T(8,128)(2,1)S(1)} %get-tuple-element.17.own), channel_id=1, source_target_pairs={{0,4},{8,12},{4,0},{12,8},{1,5},{9,13},{5,1},{13,9},{2,6},{10,14},... | collective-permute-start | bytes 344072 | tf_op jit(solution)/shard_map/ppermute | solution.py:159
  56.1 0.7 collective-permute-start.14
  56.8 11.5 %all_to_all.11 = f32[16,1,128]{2,1,0:T(1,128)S(1)} all-to-all(f32[16,1,128]{2,1,0:T(1,128)S(1)} %bitcast.5), channel_id=1, replica_groups=mesh['groups'=2,'tm'=4,'stn'=4] {'tm','stn'}, dimensions={0} | all-to-all | bytes 16384 | tf_op jit(solution)/shard_map/all_to_all | solution.py:294
  68.3 0.0 collective-permute-done.13.a
  68.3 0.0 collective-permute-done.14.b
  68.3 1.4 %shard_map.69 = (f32[32,1792]{1,0:T(8,128)}, f32[32,1792]{1,0:T(8,128)}) custom-call(f32[16,128]{1,0:T(8,128)S(1)} %bitcast.4, f32[32,1792]{1,0:T(8,128)S(1)} %get-tuple-element.12.refs_8_.field_ref, f32[32,1792]{1,0:T(8,128)S(1)} %get-tuple-element.15.image_ref, f32[32,1792]{1,0:T(8,128)S(1)} %get-tuple-element.13.refs_9_.gain_ref, ...), custom_call_target="tpu_custom_call" | custom-call | tf_op jit(solution)/shard_map/pallas_call | solution.py:23
Async XLA Ops:
  1.3 0.9 %copy-start = (f32[32,1792]{1,0:T(8,128)S(1)}, f32[32,1792]{1,0:T(8,128)}, u32[]{:S(2)}) copy-start(f32[32,1792]{1,0:T(8,128)} %field_hbm.1) | copy-start | bytes 688132
  2.3 0.7 %copy-start.1 = (s32[2,1792]{1,0:T(2,128)S(1)}, s32[2,1792]{1,0:T(2,128)}, u32[]{:S(2)}) copy-start(s32[2,1792]{1,0:T(2,128)} %mask_hbm.1) | copy-start | bytes 43012
  3.0 0.7 %copy-start.2 = (s32[2,1792]{1,0:T(2,128)S(1)}, s32[2,1792]{1,0:T(2,128)}, u32[]{:S(2)}) copy-start(s32[2,1792]{1,0:T(2,128)} %coords_hbm.1) | copy-start | bytes 43012
  4.1 6.3 %collective-permute-start = (bf16[32,1792]{1,0:T(8,128)(2,1)S(1)}, bf16[32,1792]{1,0:T(8,128)(2,1)S(1)}, u32[]{:S(2)}, u32[]{:S(2)}) collective-permute-start(bf16[32,1792]{1,0:T(8,128)(2,1)S(1)} %get-tuple-element.10.own_ref.m0), channel_id=1, source_target_pairs={{0,4},{8,12},{4,0},{12,8},{1,5},{9,13},{5,1},{13,9},{2,6},{10,14},... | collective-permute-start | bytes 344072 | tf_op jit(solution)/shard_map/ppermute | solution.py:159
  7.2 3.1 %collective-permute-start.1 = (bf16[32,1792]{1,0:T(8,128)(2,1)S(1)}, bf16[32,1792]{1,0:T(8,128)(2,1)S(1)}, u32[]{:S(2)}, u32[]{:S(2)}) collective-permute-start(bf16[32,1792]{1,0:T(8,128)(2,1)S(1)} %get-tuple-element.10.own_ref.m0), channel_id=1, source_target_pairs={{4,8},{8,4},{5,9},{9,5},{6,10},{10,6},{7,11},{11,7},{20,24},{24,20... | collective-permute-start | bytes 344072 | tf_op jit(solution)/shard_map/ppermute | solution.py:159
  10.6 4.9 %collective-permute-start.3 = (bf16[32,1792]{1,0:T(8,128)(2,1)S(1)}, bf16[32,1792]{1,0:T(8,128)(2,1)S(1)}, u32[]{:S(2)}, u32[]{:S(2)}) collective-permute-start(bf16[32,1792]{1,0:T(8,128)(2,1)S(1)} %shard_map.60.refs_0_), channel_id=1, source_target_pairs={{2,0},{3,1},{0,2},{1,3},{6,4},{7,5},{4,6},{5,7},{10,8},{11,9},{8,1... | collective-permute-start | bytes 344072 | tf_op jit(solution)/shard_map/ppermute | solution.py:169
  12.3 23.7 %collective-permute-start.2 = (bf16[32,1792]{1,0:T(8,128)(2,1)S(1)}, bf16[32,1792]{1,0:T(8,128)(2,1)S(1)}, u32[]{:S(2)}, u32[]{:S(2)}) collective-permute-start(bf16[32,1792]{1,0:T(8,128)(2,1)S(1)} %shard_map.60.refs_0_), channel_id=1, source_target_pairs={{1,0},{0,1},{3,2},{2,3},{5,4},{4,5},{7,6},{6,7},{9,8},{8,9},{11,10... | collective-permute-start | bytes 344072 | tf_op jit(solution)/shard_map/ppermute | solution.py:169
  15.4 20.6 %collective-permute-start.4 = (bf16[32,1792]{1,0:T(8,128)(2,1)S(1)}, bf16[32,1792]{1,0:T(8,128)(2,1)S(1)}, u32[]{:S(2)}, u32[]{:S(2)}) collective-permute-start(bf16[32,1792]{1,0:T(8,128)(2,1)S(1)} %collective-permute-done.3.refs_2_), channel_id=1, source_target_pairs={{1,0},{0,1},{3,2},{2,3},{5,4},{4,5},{7,6},{6,7},{9,8},{8,9},{11,10... | collective-permute-start | bytes 344072 | tf_op jit(solution)/shard_map/ppermute | solution.py:181
  15.4 3.7 %collective-permute-start.6 = (s32[2,1792]{1,0:T(2,128)S(1)}, s32[2,1792]{1,0:T(2,128)S(1)}, u32[]{:S(2)}, u32[]{:S(2)}) collective-permute-start(s32[2,1792]{1,0:T(2,128)S(1)} %get-tuple-element.11.rows_ref.cols_ref), channel_id=1, source_target_pairs={{2,0},{3,1},{0,2},{1,3},{6,4},{7,5},{4,6},{5,7},{10,8},{11,9},{8,1... | collective-permute-start | bytes 43016 | tf_op jit(solution)/shard_map/ppermute | solution.py:169
  17.1 10.5 %collective-permute-start.5 = (s32[2,1792]{1,0:T(2,128)S(1)}, s32[2,1792]{1,0:T(2,128)S(1)}, u32[]{:S(2)}, u32[]{:S(2)}) collective-permute-start(s32[2,1792]{1,0:T(2,128)S(1)} %get-tuple-element.11.rows_ref.cols_ref), channel_id=1, source_target_pairs={{1,0},{0,1},{3,2},{2,3},{5,4},{4,5},{7,6},{6,7},{9,8},{8,9},{11,10... | collective-permute-start | bytes 43016 | tf_op jit(solution)/shard_map/ppermute | solution.py:169
  19.2 12.6 %collective-permute-start.7 = (s32[2,1792]{1,0:T(2,128)S(1)}, s32[2,1792]{1,0:T(2,128)S(1)}, u32[]{:S(2)}, u32[]{:S(2)}) collective-permute-start(s32[2,1792]{1,0:T(2,128)S(1)} %collective-permute-done.6.rows_ref), channel_id=1, source_target_pairs={{1,0},{0,1},{3,2},{2,3},{5,4},{4,5},{7,6},{6,7},{9,8},{8,9},{11,10... | collective-permute-start | bytes 43016 | tf_op jit(solution)/shard_map/ppermute | solution.py:181
  40.5 7.4 %collective-permute-start.8 = (bf16[32,1792]{1,0:T(8,128)(2,1)S(1)}, bf16[32,1792]{1,0:T(8,128)(2,1)S(1)}, u32[]{:S(2)}, u32[]{:S(2)}) collective-permute-start(bf16[32,1792]{1,0:T(8,128)(2,1)S(1)} %get-tuple-element.14.refs_0_.m1), channel_id=1, source_target_pairs={{2,0},{3,1},{0,2},{1,3},{6,4},{7,5},{4,6},{5,7},{10,8},{11,9},{8,1... | collective-permute-start | bytes 344072 | tf_op jit(solution)/shard_map/ppermute | solution.py:169
  42.2 5.8 %collective-permute-start.10 = (bf16[32,1792]{1,0:T(8,128)(2,1)S(1)}, bf16[32,1792]{1,0:T(8,128)(2,1)S(1)}, u32[]{:S(2)}, u32[]{:S(2)}) collective-permute-start(bf16[32,1792]{1,0:T(8,128)(2,1)S(1)} %get-tuple-element.14.refs_0_.m1), channel_id=1, source_target_pairs={{1,0},{0,1},{3,2},{2,3},{5,4},{4,5},{7,6},{6,7},{9,8},{8,9},{11,10... | collective-permute-start | bytes 344072 | tf_op jit(solution)/shard_map/ppermute | solution.py:169
  42.5 9.1 %collective-permute-start.11 = (bf16[32,1792]{1,0:T(8,128)(2,1)S(1)}, bf16[32,1792]{1,0:T(8,128)(2,1)S(1)}, u32[]{:S(2)}, u32[]{:S(2)}) collective-permute-start(bf16[32,1792]{1,0:T(8,128)(2,1)S(1)} %get-tuple-element.14.refs_0_.m1), channel_id=1, source_target_pairs={{0,4},{8,12},{4,0},{12,8},{1,5},{9,13},{5,1},{13,9},{2,6},{10,14},... | collective-permute-start | bytes 344072 | tf_op jit(solution)/shard_map/ppermute | solution.py:159
  47.0 4.5 %collective-permute-start.12 = (bf16[32,1792]{1,0:T(8,128)(2,1)S(1)}, bf16[32,1792]{1,0:T(8,128)(2,1)S(1)}, u32[]{:S(2)}, u32[]{:S(2)}) collective-permute-start(bf16[32,1792]{1,0:T(8,128)(2,1)S(1)} %get-tuple-element.14.refs_0_.m1), channel_id=1, source_target_pairs={{4,8},{8,4},{5,9},{9,5},{6,10},{10,6},{7,11},{11,7},{20,24},{24,20... | collective-permute-start | bytes 344072 | tf_op jit(solution)/shard_map/ppermute | solution.py:159
  47.9 3.6 %collective-permute-start.9 = (bf16[32,1792]{1,0:T(8,128)(2,1)S(1)}, bf16[32,1792]{1,0:T(8,128)(2,1)S(1)}, u32[]{:S(2)}, u32[]{:S(2)}) collective-permute-start(bf16[32,1792]{1,0:T(8,128)(2,1)S(1)} %collective-permute-done.8.block), channel_id=1, source_target_pairs={{1,0},{0,1},{3,2},{2,3},{5,4},{4,5},{7,6},{6,7},{9,8},{8,9},{11,10... | collective-permute-start | bytes 344072 | tf_op jit(solution)/shard_map/ppermute | solution.py:181
  53.0 15.3 %collective-permute-start.13 = (bf16[32,1792]{1,0:T(8,128)(2,1)S(1)}, bf16[32,1792]{1,0:T(8,128)(2,1)S(1)}, u32[]{:S(2)}, u32[]{:S(2)}) collective-permute-start(bf16[32,1792]{1,0:T(8,128)(2,1)S(1)} %get-tuple-element.17.own), channel_id=1, source_target_pairs={{0,4},{8,12},{4,0},{12,8},{1,5},{9,13},{5,1},{13,9},{2,6},{10,14},... | collective-permute-start | bytes 344072 | tf_op jit(solution)/shard_map/ppermute | solution.py:159
  56.1 12.1 %collective-permute-start.14 = (bf16[32,1792]{1,0:T(8,128)(2,1)S(1)}, bf16[32,1792]{1,0:T(8,128)(2,1)S(1)}, u32[]{:S(2)}, u32[]{:S(2)}) collective-permute-start(bf16[32,1792]{1,0:T(8,128)(2,1)S(1)} %get-tuple-element.17.own), channel_id=1, source_target_pairs={{4,8},{8,4},{5,9},{9,5},{6,10},{10,6},{7,11},{11,7},{20,24},{24,20... | collective-permute-start | bytes 344072 | tf_op jit(solution)/shard_map/ppermute | solution.py:159

commit v2 on v1

--- a/solution.py
+++ b/solution.py
@@ -31,7 +31,7 @@
 
 
 def load_body(field_hbm, mask_hbm, coords_hbm, scale_hbm, field, coords, gain, masked, mask, scale, sems):
-    pairs = ((mask_hbm, mask), (scale_hbm, scale), (field_hbm, field), (coords_hbm, coords))
+    pairs = ((mask_hbm, mask), (scale_hbm, scale.at[0]), (field_hbm, field), (coords_hbm, coords))
     copies = [
         pltpu.make_async_copy(source, target, sems.at[k])
         for k, (source, target) in enumerate(pairs)
@@ -60,11 +60,11 @@
             jax.ShapeDtypeStruct(right_side.shape, jnp.float32),
             jax.ShapeDtypeStruct(right_side.shape, jnp.bfloat16),
         ),
-        (right_side, mask, coords, scale),
+        [pltpu.with_memory_space_constraint(x, pltpu.HBM) for x in (right_side, mask, coords, scale)],
         in_specs=[HBM] * 4,
         scratch=[
             pltpu.VMEM(mask.shape, mask.dtype),
-            pltpu.VMEM(scale.shape, scale.dtype),
+            pltpu.VMEM((1, *scale.shape), scale.dtype),
             pltpu.SemaphoreType.DMA((4,)),
         ],
     )
@@ -209,15 +209,19 @@
     return jnp.sum(jnp.sum(value, axis=0, keepdims=True), axis=1, keepdims=True)
 
 
-def second_body(
-    block, tile, before, field_ref, image_ref, a0, m0, b0, a1, m1, b1, spread_ref, sums_ref
-):
-    spread = tile_gain * (before[...] + product([block], [tile]))
-    spread_ref[...] = spread.astype(spread_ref.dtype)
+def second_body(block, tile, before, spread):
+    spread[...] = (tile_gain * (before[...] + product([block], [tile]))).astype(spread.dtype)
+
+
+def close_body(field_ref, image_ref, gain_ref, first_ref, own_ref, second_ref, next_ref, sums_ref):
     field, image = field_ref[...], image_ref[...]
+    spread = hour_sum(first_ref[...], own_ref[...], second_ref[...])
+    following = gain_ref[...] * spread + noise_level * image
+    next_ref[...] = following
     norm, along = sum_all(field * field), sum_all(field * image)
     guess = norm / jnp.maximum(jnp.maximum(along, noise_level * norm), 1e-30)
     near = field - guess * image
+    near_image = image - guess * following
     values = (
         norm,
         along,
@@ -225,8 +229,9 @@
         sum_all(near * near),
         sum_all(near * image),
         sum_all(image * image),
-        sum_all(hour_sum(a0[...], m0[...], b0[...]) * spread),
-        sum_all(hour_sum(a1[...], m1[...], b1[...]) * spread),
+        sum_all(near * near_image),
+        sum_all(near * following + image * near_image),
+        sum_all(image * following),
     )
     lane = lax.broadcasted_iota(jnp.int32, sums_ref.shape, 1)
     row = jnp.zeros(sums_ref.shape, jnp.float32)
@@ -235,24 +240,21 @@
     sums_ref[...] = row
 
 
-def last_body(sums_ref, field_ref, image_ref, gain_ref, a, own, b, solution_ref, residual_ref):
+def last_body(sums_ref, field_ref, image_ref, next_ref, solution_ref, residual_ref):
     sums = sums_ref[...]
-    norm, along, guess, near2, near_image, image2, cross0, cross1 = (
-        sums[:, k : k + 1] for k in range(8)
+    norm, along, guess, near2, near_image, image2, cross0, cross1, cross2 = (
+        sums[:, k : k + 1] for k in range(9)
     )
     norm_now = sum_all(norm)
     alpha = norm_now / sum_all(along)
     off = alpha - guess
     norm_next = sum_all(near2 - 2.0 * off * near_image + off * off * image2)
-    residual_image = sum_all(near_image - off * image2)
-    cross = sum_all(cross0) - alpha * sum_all(cross1)
-    product_next = residual_image - alpha * (noise_level * residual_image + cross)
+    product_next = sum_all(cross0 - off * cross1 + off * off * cross2)
     ratio = norm_next / norm_now
     alpha_next = norm_next / (product_next - ratio * norm_next / alpha)
     field, image = field_ref[...], image_ref[...]
-    second = gain_ref[...] * hour_sum(a[...], own[...], b[...]) + noise_level * image
     residual = field - alpha * image
-    change = (image - alpha * second) + ratio * image
+    change = (image - alpha * next_ref[...]) + ratio * image
     direction = residual + ratio * field
     solution_ref[...] = alpha * field + alpha_next * direction
     residual_ref[...] = residual - alpha_next * change
@@ -264,7 +266,7 @@
     block = jax.ShapeDtypeStruct(right_side.shape, jnp.bfloat16)
     wide = jax.ShapeDtypeStruct(right_side.shape, jnp.float32)
 
-    field, coords, gain, masked = load(right_side, mask, coords, station_scale[None, :])
+    field, coords, gain, masked = load(right_side, mask, coords, station_scale)
     before, after = halo(masked)
     tiles = []
     for rows in gathered(coords):
@@ -276,25 +278,19 @@
         (*gathered(smooth), *tiles, field, gain),
     )
     blocks = gathered(image_masked)
-    image_before, image_after = halo(image_masked)
     ready = min(2, count - 1)
     total = call(functools.partial(part_body, ready), wide, (*blocks[:ready], *tiles[:ready]))
     for k in range(ready, count - 1):
         total = call(more_body, wide, (blocks[k], tiles[k], total))
-    spread, sums = call(
-        second_body,
-        (block, jax.ShapeDtypeStruct((everyone, LANES), jnp.float32)),
-        (
-            *(blocks[-1], tiles[-1], total, field, image),
-            *(before, masked, after),
-            *(image_before, image_masked, image_after),
-        ),
-    )
-    last_before, last_after = halo(spread)
+    spread = call(second_body, block, (blocks[-1], tiles[-1], total))
+    before, after = halo(spread)
+    following, sums = call(
+        close_body,
+        (wide, jax.ShapeDtypeStruct((everyone, LANES), jnp.float32)),
+        (field, image, gain, before, spread, after),
+    )
     sums = lax.all_to_all(sums, ("tm", "stn"), 0, 0, tiled=True)
-    return call(
-        last_body, (wide, wide), (sums, field, image, gain, last_before, spread, last_after)
-    )
+    return call(last_body, (wide, wide), (sums, field, image, following))
 
 
 def solution(mesh):

time: 70.1 us -> 73.1 us (1.043)
  waiting for transfers between devices: 7.48 us -> 15.6 us
  local copies, waits for them, and re-layouts: 3.06 us -> 0 us
  starting transfers between devices: 18.7 us -> 16 us
  Pallas kernels: 28.2 us -> 29.2 us
    ppermute x6, waiting for transfers between devices: 4.98 us -> 9.15 us  [from_partner(): return lax.ppermute(value, 'stn', moves)]
    ppermute x6 -> x4, waiting for transfers between devices: 2.5 us -> 6.4 us  [halo(): halves.append(lax.ppermute(field, 'tm', swaps))]
    unnamed x6 -> x0, local copies, waits for them, and re-layouts: 2.36 us -> none
    ppermute x6 -> x4, starting transfers between devices: 13 us -> 10.9 us  [halo(): halves.append(lax.ppermute(field, 'tm', swaps))]
    pallas_call x11 -> x12, Pallas kernels: 28.2 us -> 29.2 us  [call(): pl.pallas_call(body, out_shape=out_shape, in_specs=in_specs or [VMEM] * l...]
  transfers between devices with their start and end apart: 15 -> 13, of which waited for: 3 -> 5; matrix products, arithmetic and copies ran while one was open for 0% -> 0% of each run, Pallas kernels for 29% -> 28%
where the time goes in v2:
time: 73.1 us; the launch traced here: 72.8 us
  Pallas kernels  29.2 us (40%)
  starting transfers between devices  16 us (22%)
  waiting for transfers between devices  15.6 us (21%)
  blocking collectives  11.3 us (15%)
  between operations  0.75 us (1%)
    pallas_call x12, Pallas kernels, call(): pl.pallas_call(body, out_shape=out_shape, in_specs=in_specs or [VMEM] * l...  29.2 us
    all_to_all x1, blocking collectives, compute(): sums = lax.all_to_all(sums, ('tm', 'stn'), 0, 0, tiled=True)  11.3 us
    ppermute x4, starting transfers between devices, halo(): halves.append(lax.ppermute(field, 'tm', swaps))  10.9 us
    ppermute x6, waiting for transfers between devices, from_partner(): return lax.ppermute(value, 'stn', moves)  9.15 us
    ppermute x4, waiting for transfers between devices, halo(): halves.append(lax.ppermute(field, 'tm', swaps))  6.4 us
    ppermute x6, starting transfers between devices, from_partner(): return lax.ppermute(value, 'stn', moves)  5.05 us
  transfers between devices with their start and end apart: 13, of which 5 were waited for; matrix products, arithmetic and copies ran while one was open for 0% of the time, Pallas kernels for 28%

profile of v2, /device:TPU:0, one launch (start us, length us, event | category | flops | bytes accessed | tf_op | source)
XLA Modules:
  0.0 72.8 jit_solution(7353301530032768090)
XLA Ops:
  0.6 1.0 %shard_map.59 = (f32[32,1792]{1,0:T(8,128)S(1)}, s32[2,1792]{1,0:T(2,128)S(1)}, f32[32,1792]{1,0:T(8,128)S(1)}, bf16[32,1792]{1,0:T(8,128)(2,1)S(1)}) custom-call(f32[32,1792]{1,0:T(8,128)} %field_hbm.1, s32[2,1792]{1,0:T(2,128)} %mask_hbm.1, s32[2,1792]{1,0:T(2,128)} %coords_hbm.1, f32[1792]{0:T(1024)} %scale_hbm.1), custom_call_target="tpu_custom_call" | custom-call | tf_op jit(solution)/shard_map/pallas_call | solution.py:23
  1.7 0.7 collective-permute-start.1
  2.4 5.9 %collective-permute-start = (bf16[32,1792]{1,0:T(8,128)(2,1)S(1)}, bf16[32,1792]{1,0:T(8,128)(2,1)S(1)}, u32[]{:S(2)}, u32[]{:S(2)}) collective-permute-start(bf16[32,1792]{1,0:T(8,128)(2,1)S(1)} %get-tuple-element.11.own_ref), channel_id=1, source_target_pairs={{0,4},{8,12},{4,0},{12,8},{1,5},{9,13},{5,1},{13,9},{2,6},{10,14},... | collective-permute-start | bytes 344072 | tf_op jit(solution)/shard_map/ppermute | solution.py:159
  8.3 0.0 collective-permute-done.1.second_ref
  8.3 2.9 %collective-permute-done.first_ref = bf16[32,1792]{1,0:T(8,128)(2,1)S(1)} collective-permute-done((bf16[32,1792]{1,0:T(8,128)(2,1)S(1)}, bf16[32,1792]{1,0:T(8,128)(2,1)S(1)}, u32[]{:S(2)}, u32[]{:S(2)}) %collective-permute-start) | collective-permute-done | bytes 114720 | tf_op jit(solution)/shard_map/ppermute | solution.py:159
  11.2 0.2 shard_map.60.refs_0_
  11.4 1.6 %collective-permute-start.3 = (bf16[32,1792]{1,0:T(8,128)(2,1)S(1)}, bf16[32,1792]{1,0:T(8,128)(2,1)S(1)}, u32[]{:S(2)}, u32[]{:S(2)}) collective-permute-start(bf16[32,1792]{1,0:T(8,128)(2,1)S(1)} %shard_map.60.refs_0_), channel_id=1, source_target_pairs={{2,0},{3,1},{0,2},{1,3},{6,4},{7,5},{4,6},{5,7},{10,8},{11,9},{8,1... | collective-permute-start | bytes 344072 | tf_op jit(solution)/shard_map/ppermute | solution.py:169
  12.9 0.0 collective-permute-start.2
  12.9 3.3 %collective-permute-done.3.refs_2_ = bf16[32,1792]{1,0:T(8,128)(2,1)S(1)} collective-permute-done((bf16[32,1792]{1,0:T(8,128)(2,1)S(1)}, bf16[32,1792]{1,0:T(8,128)(2,1)S(1)}, u32[]{:S(2)}, u32[]{:S(2)}) %collective-permute-start.3) | collective-permute-done | bytes 114720 | tf_op jit(solution)/shard_map/ppermute | solution.py:169
  16.2 0.0 collective-permute-start.4
  16.2 1.5 %collective-permute-start.6 = (s32[2,1792]{1,0:T(2,128)S(1)}, s32[2,1792]{1,0:T(2,128)S(1)}, u32[]{:S(2)}, u32[]{:S(2)}) collective-permute-start(s32[2,1792]{1,0:T(2,128)S(1)} %get-tuple-element.12.rows_ref.cols_ref), channel_id=1, source_target_pairs={{2,0},{3,1},{0,2},{1,3},{6,4},{7,5},{4,6},{5,7},{10,8},{11,9},{8,1... | collective-permute-start | bytes 43016 | tf_op jit(solution)/shard_map/ppermute | solution.py:169
  17.7 0.2 collective-permute-start.5
  18.0 2.0 %collective-permute-done.6.rows_ref = s32[2,1792]{1,0:T(2,128)S(1)} collective-permute-done((s32[2,1792]{1,0:T(2,128)S(1)}, s32[2,1792]{1,0:T(2,128)S(1)}, u32[]{:S(2)}, u32[]{:S(2)}) %collective-permute-start.6) | collective-permute-done | bytes 14368 | tf_op jit(solution)/shard_map/ppermute | solution.py:169
  20.0 0.0 collective-permute-start.7
  20.0 4.2 %shard_map.61.refs_4_.refs_2_ = bf16[1792,1792]{1,0:T(8,128)(2,1)S(1)} custom-call(s32[2,1792]{1,0:T(2,128)S(1)} %get-tuple-element.12.rows_ref.cols_ref, s32[2,1792]{1,0:T(2,128)S(1)} %get-tuple-element.12.rows_ref.cols_ref), custom_call_target="tpu_custom_call" | custom-call | tf_op jit(solution)/shard_map/pallas_call | solution.py:23
  24.2 4.2 %shard_map.63.refs_6_.tile = bf16[1792,1792]{1,0:T(8,128)(2,1)S(1)} custom-call(s32[2,1792]{1,0:T(2,128)S(1)} %collective-permute-done.6.rows_ref, s32[2,1792]{1,0:T(2,128)S(1)} %get-tuple-element.12.rows_ref.cols_ref), custom_call_target="tpu_custom_call" | custom-call | tf_op jit(solution)/shard_map/pallas_call | solution.py:23
  28.4 0.0 collective-permute-done.5.rows_ref
  28.4 4.2 %shard_map.62.refs_5_.refs_3_ = bf16[1792,1792]{1,0:T(8,128)(2,1)S(1)} custom-call(s32[2,1792]{1,0:T(2,128)S(1)} %collective-permute-done.5.rows_ref, s32[2,1792]{1,0:T(2,128)S(1)} %get-tuple-element.12.rows_ref.cols_ref), custom_call_target="tpu_custom_call" | custom-call | tf_op jit(solution)/shard_map/pallas_call | solution.py:23
  32.6 0.0 collective-permute-done.7.rows_ref
  32.6 4.4 %shard_map.64.refs_7_.tile = bf16[1792,1792]{1,0:T(8,128)(2,1)S(1)} custom-call(s32[2,1792]{1,0:T(2,128)S(1)} %collective-permute-done.7.rows_ref, s32[2,1792]{1,0:T(2,128)S(1)} %get-tuple-element.12.rows_ref.cols_ref), custom_call_target="tpu_custom_call" | custom-call | tf_op jit(solution)/shard_map/pallas_call | solution.py:23
  37.0 0.0 collective-permute-done.2.refs_1_
  37.0 0.0 collective-permute-done.4.refs_3_
  37.0 4.5 %shard_map.65 = (f32[32,1792]{1,0:T(8,128)S(1)}, bf16[32,1792]{1,0:T(8,128)(2,1)S(1)}) custom-call(bf16[32,1792]{1,0:T(8,128)(2,1)S(1)} %shard_map.60.refs_0_, bf16[32,1792]{1,0:T(8,128)(2,1)S(1)} %collective-permute-done.2.refs_1_, bf16[32,1792]{1,0:T(8,128)(2,1)S(1)} %collective-permute-done.3.refs_2_, ...), custom_call_target="tpu_custom_call" | custom-call | tf_op jit(solution)/shard_map/pallas_call | solution.py:23
  41.5 1.6 %collective-permute-start.8 = (bf16[32,1792]{1,0:T(8,128)(2,1)S(1)}, bf16[32,1792]{1,0:T(8,128)(2,1)S(1)}, u32[]{:S(2)}, u32[]{:S(2)}) collective-permute-start(bf16[32,1792]{1,0:T(8,128)(2,1)S(1)} %get-tuple-element.15.refs_0_), channel_id=1, source_target_pairs={{2,0},{3,1},{0,2},{1,3},{6,4},{7,5},{4,6},{5,7},{10,8},{11,9},{8,1... | collective-permute-start | bytes 344072 | tf_op jit(solution)/shard_map/ppermute | solution.py:169
  43.0 0.2 collective-permute-start.10
  43.3 3.8 %collective-permute-done.8.block = bf16[32,1792]{1,0:T(8,128)(2,1)S(1)} collective-permute-done((bf16[32,1792]{1,0:T(8,128)(2,1)S(1)}, bf16[32,1792]{1,0:T(8,128)(2,1)S(1)}, u32[]{:S(2)}, u32[]{:S(2)}) %collective-permute-start.8) | collective-permute-done | bytes 114720 | tf_op jit(solution)/shard_map/ppermute | solution.py:169
  47.1 0.0 collective-permute-start.9
  47.1 0.0 collective-permute-done.10.refs_1_
  47.1 2.3 %shard_map.66.before = f32[32,1792]{1,0:T(8,128)S(1)} custom-call(bf16[32,1792]{1,0:T(8,128)(2,1)S(1)} %get-tuple-element.15.refs_0_, bf16[32,1792]{1,0:T(8,128)(2,1)S(1)} %collective-permute-done.10.refs_1_, bf16[1792,1792]{1,0:T(8,128)(2,1)S(1)} %shard_map.61.refs_4_.refs_2_, bf16[1792,1792]{1,0:T(8,128)(2,1)S(1)} %shard_map.62.refs_5_.refs_3_), custom_call_target="tpu_custom_call" | custom-call | tf_op jit(solution)/shard_map/pallas_call | solution.py:23
  49.4 1.2 %shard_map.67.before = f32[32,1792]{1,0:T(8,128)S(1)} custom-call(bf16[32,1792]{1,0:T(8,128)(2,1)S(1)} %collective-permute-done.8.block, bf16[1792,1792]{1,0:T(8,128)(2,1)S(1)} %shard_map.63.refs_6_.tile, f32[32,1792]{1,0:T(8,128)S(1)} %shard_map.66.before), custom_call_target="tpu_custom_call" | custom-call | tf_op jit(solution)/shard_map/pallas_call | solution.py:23
  50.6 0.0 collective-permute-done.9.block
  50.6 1.2 %shard_map.68.own_ref = bf16[32,1792]{1,0:T(8,128)(2,1)S(1)} custom-call(bf16[32,1792]{1,0:T(8,128)(2,1)S(1)} %collective-permute-done.9.block, bf16[1792,1792]{1,0:T(8,128)(2,1)S(1)} %shard_map.64.refs_7_.tile, f32[32,1792]{1,0:T(8,128)S(1)} %shard_map.67.before), custom_call_target="tpu_custom_call" | custom-call | tf_op jit(solution)/shard_map/pallas_call | solution.py:23
  51.9 0.7 collective-permute-start.12
  52.5 3.7 %collective-permute-start.11 = (bf16[32,1792]{1,0:T(8,128)(2,1)S(1)}, bf16[32,1792]{1,0:T(8,128)(2,1)S(1)}, u32[]{:S(2)}, u32[]{:S(2)}) collective-permute-start(bf16[32,1792]{1,0:T(8,128)(2,1)S(1)} %shard_map.68.own_ref), channel_id=1, source_target_pairs={{0,4},{8,12},{4,0},{12,8},{1,5},{9,13},{5,1},{13,9},{2,6},{10,14},... | collective-permute-start | bytes 344072 | tf_op jit(solution)/shard_map/ppermute | solution.py:159
  56.2 0.0 collective-permute-done.12.second_ref
  56.2 3.5 %collective-permute-done.11.first_ref = bf16[32,1792]{1,0:T(8,128)(2,1)S(1)} collective-permute-done((bf16[32,1792]{1,0:T(8,128)(2,1)S(1)}, bf16[32,1792]{1,0:T(8,128)(2,1)S(1)}, u32[]{:S(2)}, u32[]{:S(2)}) %collective-permute-start.11) | collective-permute-done | bytes 114720 | tf_op jit(solution)/shard_map/ppermute | solution.py:159
  59.8 0.5 shard_map.69
  60.2 11.3 %all_to_all.11 = f32[16,1,128]{2,1,0:T(1,128)S(1)} all-to-all(f32[16,1,128]{2,1,0:T(1,128)S(1)} %bitcast.5), channel_id=1, replica_groups=mesh['groups'=2,'tm'=4,'stn'=4] {'tm','stn'}, dimensions={0} | all-to-all | bytes 16384 | tf_op jit(solution)/shard_map/all_to_all | solution.py:292
  71.5 1.2 %shard_map.70 = (f32[32,1792]{1,0:T(8,128)}, f32[32,1792]{1,0:T(8,128)}) custom-call(f32[16,128]{1,0:T(8,128)S(1)} %bitcast.4, f32[32,1792]{1,0:T(8,128)S(1)} %get-tuple-element.10.refs_8_.field_ref, f32[32,1792]{1,0:T(8,128)S(1)} %get-tuple-element.14.image_ref, f32[32,1792]{1,0:T(8,128)S(1)} %get-tuple-element.17.next_ref), custom_call_target="tpu_custom_call" | custom-call | tf_op jit(solution)/shard_map/pallas_call | solution.py:23
Async XLA Ops:
  1.7 6.6 %collective-permute-start.1 = (bf16[32,1792]{1,0:T(8,128)(2,1)S(1)}, bf16[32,1792]{1,0:T(8,128)(2,1)S(1)}, u32[]{:S(2)}, u32[]{:S(2)}) collective-permute-start(bf16[32,1792]{1,0:T(8,128)(2,1)S(1)} %get-tuple-element.11.own_ref), channel_id=1, source_target_pairs={{4,8},{8,4},{5,9},{9,5},{6,10},{10,6},{7,11},{11,7},{20,24},{24,20... | collective-permute-start | bytes 344072 | tf_op jit(solution)/shard_map/ppermute | solution.py:159
  2.4 8.8 %collective-permute-start = (bf16[32,1792]{1,0:T(8,128)(2,1)S(1)}, bf16[32,1792]{1,0:T(8,128)(2,1)S(1)}, u32[]{:S(2)}, u32[]{:S(2)}) collective-permute-start(bf16[32,1792]{1,0:T(8,128)(2,1)S(1)} %get-tuple-element.11.own_ref), channel_id=1, source_target_pairs={{0,4},{8,12},{4,0},{12,8},{1,5},{9,13},{5,1},{13,9},{2,6},{10,14},... | collective-permute-start | bytes 344072 | tf_op jit(solution)/shard_map/ppermute | solution.py:159
  11.4 4.9 %collective-permute-start.3 = (bf16[32,1792]{1,0:T(8,128)(2,1)S(1)}, bf16[32,1792]{1,0:T(8,128)(2,1)S(1)}, u32[]{:S(2)}, u32[]{:S(2)}) collective-permute-start(bf16[32,1792]{1,0:T(8,128)(2,1)S(1)} %shard_map.60.refs_0_), channel_id=1, source_target_pairs={{2,0},{3,1},{0,2},{1,3},{6,4},{7,5},{4,6},{5,7},{10,8},{11,9},{8,1... | collective-permute-start | bytes 344072 | tf_op jit(solution)/shard_map/ppermute | solution.py:169
  12.9 24.0 %collective-permute-start.2 = (bf16[32,1792]{1,0:T(8,128)(2,1)S(1)}, bf16[32,1792]{1,0:T(8,128)(2,1)S(1)}, u32[]{:S(2)}, u32[]{:S(2)}) collective-permute-start(bf16[32,1792]{1,0:T(8,128)(2,1)S(1)} %shard_map.60.refs_0_), channel_id=1, source_target_pairs={{1,0},{0,1},{3,2},{2,3},{5,4},{4,5},{7,6},{6,7},{9,8},{8,9},{11,10... | collective-permute-start | bytes 344072 | tf_op jit(solution)/shard_map/ppermute | solution.py:169
  16.2 20.7 %collective-permute-start.4 = (bf16[32,1792]{1,0:T(8,128)(2,1)S(1)}, bf16[32,1792]{1,0:T(8,128)(2,1)S(1)}, u32[]{:S(2)}, u32[]{:S(2)}) collective-permute-start(bf16[32,1792]{1,0:T(8,128)(2,1)S(1)} %collective-permute-done.3.refs_2_), channel_id=1, source_target_pairs={{1,0},{0,1},{3,2},{2,3},{5,4},{4,5},{7,6},{6,7},{9,8},{8,9},{11,10... | collective-permute-start | bytes 344072 | tf_op jit(solution)/shard_map/ppermute | solution.py:181
  16.2 3.7 %collective-permute-start.6 = (s32[2,1792]{1,0:T(2,128)S(1)}, s32[2,1792]{1,0:T(2,128)S(1)}, u32[]{:S(2)}, u32[]{:S(2)}) collective-permute-start(s32[2,1792]{1,0:T(2,128)S(1)} %get-tuple-element.12.rows_ref.cols_ref), channel_id=1, source_target_pairs={{2,0},{3,1},{0,2},{1,3},{6,4},{7,5},{4,6},{5,7},{10,8},{11,9},{8,1... | collective-permute-start | bytes 43016 | tf_op jit(solution)/shard_map/ppermute | solution.py:169
  17.7 10.6 %collective-permute-start.5 = (s32[2,1792]{1,0:T(2,128)S(1)}, s32[2,1792]{1,0:T(2,128)S(1)}, u32[]{:S(2)}, u32[]{:S(2)}) collective-permute-start(s32[2,1792]{1,0:T(2,128)S(1)} %get-tuple-element.12.rows_ref.cols_ref), channel_id=1, source_target_pairs={{1,0},{0,1},{3,2},{2,3},{5,4},{4,5},{7,6},{6,7},{9,8},{8,9},{11,10... | collective-permute-start | bytes 43016 | tf_op jit(solution)/shard_map/ppermute | solution.py:169
  20.0 12.6 %collective-permute-start.7 = (s32[2,1792]{1,0:T(2,128)S(1)}, s32[2,1792]{1,0:T(2,128)S(1)}, u32[]{:S(2)}, u32[]{:S(2)}) collective-permute-start(s32[2,1792]{1,0:T(2,128)S(1)} %collective-permute-done.6.rows_ref), channel_id=1, source_target_pairs={{1,0},{0,1},{3,2},{2,3},{5,4},{4,5},{7,6},{6,7},{9,8},{8,9},{11,10... | collective-permute-start | bytes 43016 | tf_op jit(solution)/shard_map/ppermute | solution.py:181
  41.5 5.6 %collective-permute-start.8 = (bf16[32,1792]{1,0:T(8,128)(2,1)S(1)}, bf16[32,1792]{1,0:T(8,128)(2,1)S(1)}, u32[]{:S(2)}, u32[]{:S(2)}) collective-permute-start(bf16[32,1792]{1,0:T(8,128)(2,1)S(1)} %get-tuple-element.15.refs_0_), channel_id=1, source_target_pairs={{2,0},{3,1},{0,2},{1,3},{6,4},{7,5},{4,6},{5,7},{10,8},{11,9},{8,1... | collective-permute-start | bytes 344072 | tf_op jit(solution)/shard_map/ppermute | solution.py:169
  43.0 4.1 %collective-permute-start.10 = (bf16[32,1792]{1,0:T(8,128)(2,1)S(1)}, bf16[32,1792]{1,0:T(8,128)(2,1)S(1)}, u32[]{:S(2)}, u32[]{:S(2)}) collective-permute-start(bf16[32,1792]{1,0:T(8,128)(2,1)S(1)} %get-tuple-element.15.refs_0_), channel_id=1, source_target_pairs={{1,0},{0,1},{3,2},{2,3},{5,4},{4,5},{7,6},{6,7},{9,8},{8,9},{11,10... | collective-permute-start | bytes 344072 | tf_op jit(solution)/shard_map/ppermute | solution.py:169
  47.1 3.5 %collective-permute-start.9 = (bf16[32,1792]{1,0:T(8,128)(2,1)S(1)}, bf16[32,1792]{1,0:T(8,128)(2,1)S(1)}, u32[]{:S(2)}, u32[]{:S(2)}) collective-permute-start(bf16[32,1792]{1,0:T(8,128)(2,1)S(1)} %collective-permute-done.8.block), channel_id=1, source_target_pairs={{1,0},{0,1},{3,2},{2,3},{5,4},{4,5},{7,6},{6,7},{9,8},{8,9},{11,10... | collective-permute-start | bytes 344072 | tf_op jit(solution)/shard_map/ppermute | solution.py:181
  51.9 4.3 %collective-permute-start.12 = (bf16[32,1792]{1,0:T(8,128)(2,1)S(1)}, bf16[32,1792]{1,0:T(8,128)(2,1)S(1)}, u32[]{:S(2)}, u32[]{:S(2)}) collective-permute-start(bf16[32,1792]{1,0:T(8,128)(2,1)S(1)} %shard_map.68.own_ref), channel_id=1, source_target_pairs={{4,8},{8,4},{5,9},{9,5},{6,10},{10,6},{7,11},{11,7},{20,24},{24,20... | collective-permute-start | bytes 344072 | tf_op jit(solution)/shard_map/ppermute | solution.py:159
  52.5 7.2 %collective-permute-start.11 = (bf16[32,1792]{1,0:T(8,128)(2,1)S(1)}, bf16[32,1792]{1,0:T(8,128)(2,1)S(1)}, u32[]{:S(2)}, u32[]{:S(2)}) collective-permute-start(bf16[32,1792]{1,0:T(8,128)(2,1)S(1)} %shard_map.68.own_ref), channel_id=1, source_target_pairs={{0,4},{8,12},{4,0},{12,8},{1,5},{9,13},{5,1},{13,9},{2,6},{10,14},... | collective-permute-start | bytes 344072 | tf_op jit(solution)/shard_map/ppermute | solution.py:159

commit v3 on v1

--- a/solution.py
+++ b/solution.py
@@ -31,7 +31,7 @@
 
 
 def load_body(field_hbm, mask_hbm, coords_hbm, scale_hbm, field, coords, gain, masked, mask, scale, sems):
-    pairs = ((mask_hbm, mask), (scale_hbm, scale), (field_hbm, field), (coords_hbm, coords))
+    pairs = ((mask_hbm, mask), (scale_hbm, scale.at[0]), (field_hbm, field), (coords_hbm, coords))
     copies = [
         pltpu.make_async_copy(source, target, sems.at[k])
         for k, (source, target) in enumerate(pairs)
@@ -60,11 +60,11 @@
             jax.ShapeDtypeStruct(right_side.shape, jnp.float32),
             jax.ShapeDtypeStruct(right_side.shape, jnp.bfloat16),
         ),
-        (right_side, mask, coords, scale),
+        [pltpu.with_memory_space_constraint(x, pltpu.HBM) for x in (right_side, mask, coords, scale)],
         in_specs=[HBM] * 4,
         scratch=[
             pltpu.VMEM(mask.shape, mask.dtype),
-            pltpu.VMEM(scale.shape, scale.dtype),
+            pltpu.VMEM((1, *scale.shape), scale.dtype),
             pltpu.SemaphoreType.DMA((4,)),
         ],
     )
@@ -83,39 +83,55 @@
 
 
 def step_of(extent):
-    for step in (896, 512, 256, 128, 64, 32, 16):
+    for step in (256, 128, 64, 32, 16):
         if extent % step == 0:
             return step
     return extent
 
 
-def tile_body(rows_ref, cols_ref, tile_ref, row_features, col_features):
+def tile_body(rows_ref, cols_ref, *refs):
+    *given, row_features, col_features = refs
+    if len(given) == 1:
+        (tile_ref,), blocks, befores, total_ref, total = given, (), (), None, None
+    else:
+        *given, tile_ref, total_ref = given
+        pairs = len(given) // 2
+        blocks, befores = given[:pairs], given[pairs : 2 * pairs]
+        total = given[2 * pairs] if len(given) % 2 else None
     row_features[...] = features(rows_ref[...], True).T.astype(jnp.bfloat16)
     col_features[...] = features(cols_ref[...], False).astype(jnp.bfloat16)
-    step = step_of(tile_ref.shape[0])
-
-    def body(index, carry):
-        at = pl.ds(pl.multiple_of(index * step, step), step)
+    extent = tile_ref.shape[0]
+    step = step_of(extent)
+    for start in range(0, extent, step):
+        at = pl.ds(start, step)
         square = jnp.dot(
             row_features[at, :], col_features[...], preferred_element_type=jnp.float32
         )
         distance = square * lax.rsqrt(jnp.maximum(square, 1e-20))
         decay = jnp.exp2(distance * (-slope * math.log2(math.e)))
         tile_ref[at, :] = ((1.0 / slope + distance) * decay).astype(jnp.bfloat16)
-        return carry
-
-    lax.fori_loop(0, tile_ref.shape[0] // step, body, 0)
+        for index, (block, before) in enumerate(zip(blocks, befores)):
+            part = jnp.dot(block[:, at], before[at, :], preferred_element_type=jnp.float32)
+            if index or start:
+                part += total_ref[...]
+            elif total is not None:
+                part += total[...]
+            total_ref[...] = part
 
 
 tile_gain = slope / kernel_norm
 
 
-def matern_tile(rows, cols):
+def matern_tile(rows, cols, blocks=(), tiles=(), total=None):
     extent, width = rows.shape[1], cols.shape[1]
+    tile = jax.ShapeDtypeStruct((extent, width), jnp.bfloat16)
+    out = tile
+    if blocks:
+        out = (tile, jax.ShapeDtypeStruct((blocks[0].shape[0], width), jnp.float32))
     return call(
         tile_body,
-        jax.ShapeDtypeStruct((extent, width), jnp.bfloat16),
-        (rows, cols),
+        out,
+        (rows, cols, *blocks, *tiles, *(() if total is None else (total,))),
         scratch=[pltpu.VMEM((extent, 8), jnp.bfloat16), pltpu.VMEM((8, width), jnp.bfloat16)],
     )
 
@@ -191,8 +207,8 @@
 
 def first_body(count, *refs):
     blocks, tiles = refs[:count], refs[count : 2 * count]
-    field, gain, image, masked = refs[2 * count :]
-    spread = tile_gain * product(blocks, tiles)
+    total, field, gain, image, masked = refs[2 * count :]
+    spread = tile_gain * (total[...] + product(blocks, tiles))
     image[...] = gain[...] * spread + noise_level * field[...]
     masked[...] = (gain[...] * image[...]).astype(masked.dtype)
 
@@ -264,16 +280,25 @@
     block = jax.ShapeDtypeStruct(right_side.shape, jnp.bfloat16)
     wide = jax.ShapeDtypeStruct(right_side.shape, jnp.float32)
 
-    field, coords, gain, masked = load(right_side, mask, coords, station_scale[None, :])
+    field, coords, gain, masked = load(right_side, mask, coords, station_scale)
     before, after = halo(masked)
-    tiles = []
-    for rows in gathered(coords):
-        tiles.append(matern_tile(rows, coords))
     smooth = call(smooth_body, block, (before, masked, after))
+    rows, ring = gathered(coords), gathered(smooth)
+    tiles, total, used = [], None, 0
+    for k in range(count):
+        ready = k
+        if ready > used:
+            tile, total = matern_tile(rows[k], coords, ring[used:ready], tiles[used:ready], total)
+        else:
+            tile = matern_tile(rows[k], coords)
+        used = max(used, ready)
+        tiles.append(tile)
+    if total is None:
+        total = jnp.zeros(right_side.shape, jnp.float32)
     image, image_masked = call(
-        functools.partial(first_body, count),
+        functools.partial(first_body, count - used),
         (wide, block),
-        (*gathered(smooth), *tiles, field, gain),
+        (*ring[used:], *tiles[used:], total, field, gain),
     )
     blocks = gathered(image_masked)
     image_before, image_after = halo(image_masked)

time: 70.1 us -> 63.5 us (0.906)
  Pallas kernels: 28.2 us -> 24.8 us
  local copies, waits for them, and re-layouts: 3.06 us -> 0 us
    pallas_call x11, Pallas kernels: 28.2 us -> 24.8 us  [call(): pl.pallas_call(body, out_shape=out_shape, in_specs=in_specs or [VMEM] * l...]
    unnamed x6 -> x0, local copies, waits for them, and re-layouts: 2.36 us -> none
    broadcast_in_dim x1 -> x0, local copies, waits for them, and re-layouts: 0.7 us -> none  [compute(): station_scale[None, :]]
  transfers between devices with their start and end apart: 15 -> 15, of which waited for: 3 -> 3; matrix products, arithmetic and copies ran while one was open for 0% -> 0% of each run, Pallas kernels for 29% -> 31%
where the time goes in v3:
time: 63.5 us; the launch traced here: 63.2 us
  Pallas kernels  24.8 us (39%)
  starting transfers between devices  18.5 us (29%)
  blocking collectives  11.6 us (18%)
  waiting for transfers between devices  7.48 us (12%)
  between operations  0.79 us (1%)
    pallas_call x11, Pallas kernels, call(): pl.pallas_call(body, out_shape=out_shape, in_specs=in_specs or [VMEM] * l...  24.8 us
    ppermute x6, starting transfers between devices, halo(): halves.append(lax.ppermute(field, 'tm', swaps))  12.8 us
    all_to_all x1, blocking collectives, compute(): sums = lax.all_to_all(sums, ('tm', 'stn'), 0, 0, tiled=True)  11.6 us
    ppermute x6, starting transfers between devices, from_partner(): return lax.ppermute(value, 'stn', moves)  5.57 us
    ppermute x6, waiting for transfers between devices, from_partner(): return lax.ppermute(value, 'stn', moves)  4.97 us
    ppermute x6, waiting for transfers between devices, halo(): halves.append(lax.ppermute(field, 'tm', swaps))  2.5 us
  transfers between devices with their start and end apart: 15, of which 3 were waited for; matrix products, arithmetic and copies ran while one was open for 0% of the time, Pallas kernels for 31%

profile of v3, /device:TPU:0, one launch (start us, length us, event | category | flops | bytes accessed | tf_op | source)
XLA Modules:
  0.0 63.2 jit_solution(8914959414631581795)
XLA Ops:
  0.6 1.0 %shard_map.59 = (f32[32,1792]{1,0:T(8,128)S(1)}, s32[2,1792]{1,0:T(2,128)S(1)}, f32[32,1792]{1,0:T(8,128)S(1)}, bf16[32,1792]{1,0:T(8,128)(2,1)S(1)}) custom-call(f32[32,1792]{1,0:T(8,128)} %field_hbm.1, s32[2,1792]{1,0:T(2,128)} %mask_hbm.1, s32[2,1792]{1,0:T(2,128)} %coords_hbm.1, f32[1792]{0:T(1024)} %scale_hbm.1), custom_call_target="tpu_custom_call" | custom-call | tf_op jit(solution)/shard_map/pallas_call | solution.py:23
  1.7 3.1 %collective-permute-start = (bf16[32,1792]{1,0:T(8,128)(2,1)S(1)}, bf16[32,1792]{1,0:T(8,128)(2,1)S(1)}, u32[]{:S(2)}, u32[]{:S(2)}) collective-permute-start(bf16[32,1792]{1,0:T(8,128)(2,1)S(1)} %get-tuple-element.16.own_ref.m0), channel_id=1, source_target_pairs={{0,4},{8,12},{4,0},{12,8},{1,5},{9,13},{5,1},{13,9},{2,6},{10,14},... | collective-permute-start | bytes 344072 | tf_op jit(solution)/shard_map/ppermute | solution.py:175
  4.8 0.7 %collective-permute-start.1 = (bf16[32,1792]{1,0:T(8,128)(2,1)S(1)}, bf16[32,1792]{1,0:T(8,128)(2,1)S(1)}, u32[]{:S(2)}, u32[]{:S(2)}) collective-permute-start(bf16[32,1792]{1,0:T(8,128)(2,1)S(1)} %get-tuple-element.16.own_ref.m0), channel_id=1, source_target_pairs={{4,8},{8,4},{5,9},{9,5},{6,10},{10,6},{7,11},{11,7},{20,24},{24,20... | collective-permute-start | bytes 344072 | tf_op jit(solution)/shard_map/ppermute | solution.py:175
  5.5 2.5 %collective-permute-done.first_ref.a0 = bf16[32,1792]{1,0:T(8,128)(2,1)S(1)} collective-permute-done((bf16[32,1792]{1,0:T(8,128)(2,1)S(1)}, bf16[32,1792]{1,0:T(8,128)(2,1)S(1)}, u32[]{:S(2)}, u32[]{:S(2)}) %collective-permute-start) | collective-permute-done | bytes 114720 | tf_op jit(solution)/shard_map/ppermute | solution.py:175
  7.9 0.0 collective-permute-done.1.second_ref.b0
  7.9 0.2 shard_map.60.refs_0_
  8.2 1.7 %collective-permute-start.2 = (bf16[32,1792]{1,0:T(8,128)(2,1)S(1)}, bf16[32,1792]{1,0:T(8,128)(2,1)S(1)}, u32[]{:S(2)}, u32[]{:S(2)}) collective-permute-start(bf16[32,1792]{1,0:T(8,128)(2,1)S(1)} %shard_map.60.refs_0_), channel_id=1, source_target_pairs={{2,0},{3,1},{0,2},{1,3},{6,4},{7,5},{4,6},{5,7},{10,8},{11,9},{8,1... | collective-permute-start | bytes 344072 | tf_op jit(solution)/shard_map/ppermute | solution.py:185
  9.9 0.0 collective-permute-start.6
  9.9 3.1 %collective-permute-done.2.refs_0_ = bf16[32,1792]{1,0:T(8,128)(2,1)S(1)} collective-permute-done((bf16[32,1792]{1,0:T(8,128)(2,1)S(1)}, bf16[32,1792]{1,0:T(8,128)(2,1)S(1)}, u32[]{:S(2)}, u32[]{:S(2)}) %collective-permute-start.2) | collective-permute-done | bytes 114720 | tf_op jit(solution)/shard_map/ppermute | solution.py:185
  13.0 0.0 collective-permute-start.3
  13.0 1.7 %collective-permute-start.4 = (s32[2,1792]{1,0:T(2,128)S(1)}, s32[2,1792]{1,0:T(2,128)S(1)}, u32[]{:S(2)}, u32[]{:S(2)}) collective-permute-start(s32[2,1792]{1,0:T(2,128)S(1)} %get-tuple-element.17.rows_ref.cols_ref), channel_id=1, source_target_pairs={{2,0},{3,1},{0,2},{1,3},{6,4},{7,5},{4,6},{5,7},{10,8},{11,9},{8,1... | collective-permute-start | bytes 43016 | tf_op jit(solution)/shard_map/ppermute | solution.py:185
  14.7 0.2 collective-permute-start.7
  14.9 1.8 %collective-permute-done.4.rows_ref = s32[2,1792]{1,0:T(2,128)S(1)} collective-permute-done((s32[2,1792]{1,0:T(2,128)S(1)}, s32[2,1792]{1,0:T(2,128)S(1)}, u32[]{:S(2)}, u32[]{:S(2)}) %collective-permute-start.4) | collective-permute-done | bytes 14368 | tf_op jit(solution)/shard_map/ppermute | solution.py:185
  16.7 0.0 collective-permute-start.5
  16.8 4.1 %shard_map.61.refs_1_.refs_2_ = bf16[1792,1792]{1,0:T(8,128)(2,1)S(1)} custom-call(s32[2,1792]{1,0:T(2,128)S(1)} %get-tuple-element.17.rows_ref.cols_ref, s32[2,1792]{1,0:T(2,128)S(1)} %get-tuple-element.17.rows_ref.cols_ref), custom_call_target="tpu_custom_call" | custom-call | tf_op jit(solution)/shard_map/pallas_call | solution.py:23
  20.9 0.0 collective-permute-done.7.rows_ref
  20.9 3.9 %shard_map.62 = (bf16[1792,1792]{1,0:T(8,128)(2,1)S(1)}, f32[32,1792]{1,0:T(8,128)S(1)}) custom-call(s32[2,1792]{1,0:T(2,128)S(1)} %collective-permute-done.7.rows_ref, s32[2,1792]{1,0:T(2,128)S(1)} %get-tuple-element.17.rows_ref.cols_ref, bf16[32,1792]{1,0:T(8,128)(2,1)S(1)} %shard_map.60.refs_0_, bf16[1792,1792]{1,0:T(8,128)(2,1)S(1)} %shard_map.61.refs_1_.refs_2_), custom_call_target="tpu_custom_call" | custom-call | tf_op jit(solution)/shard_map/pallas_call | solution.py:23
  24.7 0.0 collective-permute-done.6.refs_0_
  24.8 4.1 %shard_map.63 = (bf16[1792,1792]{1,0:T(8,128)(2,1)S(1)}, f32[32,1792]{1,0:T(8,128)S(1)}) custom-call(s32[2,1792]{1,0:T(2,128)S(1)} %collective-permute-done.4.rows_ref, s32[2,1792]{1,0:T(2,128)S(1)} %get-tuple-element.17.rows_ref.cols_ref, bf16[32,1792]{1,0:T(8,128)(2,1)S(1)} %collective-permute-done.6.refs_0_, ...), custom_call_target="tpu_custom_call" | custom-call | tf_op jit(solution)/shard_map/pallas_call | solution.py:23
  28.8 0.0 collective-permute-done.5.rows_ref
  28.8 3.9 %shard_map.64 = (bf16[1792,1792]{1,0:T(8,128)(2,1)S(1)}, f32[32,1792]{1,0:T(8,128)S(1)}) custom-call(s32[2,1792]{1,0:T(2,128)S(1)} %collective-permute-done.5.rows_ref, s32[2,1792]{1,0:T(2,128)S(1)} %get-tuple-element.17.rows_ref.cols_ref, bf16[32,1792]{1,0:T(8,128)(2,1)S(1)} %collective-permute-done.2.refs_0_, ...), custom_call_target="tpu_custom_call" | custom-call | tf_op jit(solution)/shard_map/pallas_call | solution.py:23
  32.7 0.0 collective-permute-done.3.refs_0_
  32.7 1.2 %shard_map.65 = (f32[32,1792]{1,0:T(8,128)S(1)}, bf16[32,1792]{1,0:T(8,128)(2,1)S(1)}) custom-call(bf16[32,1792]{1,0:T(8,128)(2,1)S(1)} %collective-permute-done.3.refs_0_, bf16[1792,1792]{1,0:T(8,128)(2,1)S(1)} %get-tuple-element.22.refs_1_.tile, f32[32,1792]{1,0:T(8,128)S(1)} %get-tuple-element.23.refs_2_, ...), custom_call_target="tpu_custom_call" | custom-call | tf_op jit(solution)/shard_map/pallas_call | solution.py:23
  34.0 1.7 %collective-permute-start.8 = (bf16[32,1792]{1,0:T(8,128)(2,1)S(1)}, bf16[32,1792]{1,0:T(8,128)(2,1)S(1)}, u32[]{:S(2)}, u32[]{:S(2)}) collective-permute-start(bf16[32,1792]{1,0:T(8,128)(2,1)S(1)} %get-tuple-element.26.refs_0_.m1), channel_id=1, source_target_pairs={{2,0},{3,1},{0,2},{1,3},{6,4},{7,5},{4,6},{5,7},{10,8},{11,9},{8,1... | collective-permute-start | bytes 344072 | tf_op jit(solution)/shard_map/ppermute | solution.py:185
  35.7 0.2 collective-permute-start.10
  35.9 4.6 %collective-permute-start.11 = (bf16[32,1792]{1,0:T(8,128)(2,1)S(1)}, bf16[32,1792]{1,0:T(8,128)(2,1)S(1)}, u32[]{:S(2)}, u32[]{:S(2)}) collective-permute-start(bf16[32,1792]{1,0:T(8,128)(2,1)S(1)} %get-tuple-element.26.refs_0_.m1), channel_id=1, source_target_pairs={{0,4},{8,12},{4,0},{12,8},{1,5},{9,13},{5,1},{13,9},{2,6},{10,14},... | collective-permute-start | bytes 344072 | tf_op jit(solution)/shard_map/ppermute | solution.py:175
  40.5 0.7 %collective-permute-start.12 = (bf16[32,1792]{1,0:T(8,128)(2,1)S(1)}, bf16[32,1792]{1,0:T(8,128)(2,1)S(1)}, u32[]{:S(2)}, u32[]{:S(2)}) collective-permute-start(bf16[32,1792]{1,0:T(8,128)(2,1)S(1)} %get-tuple-element.26.refs_0_.m1), channel_id=1, source_target_pairs={{4,8},{8,4},{5,9},{9,5},{6,10},{10,6},{7,11},{11,7},{20,24},{24,20... | collective-permute-start | bytes 344072 | tf_op jit(solution)/shard_map/ppermute | solution.py:175
  41.2 0.0 collective-permute-done.8.block
  41.2 0.1 collective-permute-start.9
  41.3 0.0 collective-permute-done.10.refs_1_
  41.3 2.3 %shard_map.66.before = f32[32,1792]{1,0:T(8,128)S(1)} custom-call(bf16[32,1792]{1,0:T(8,128)(2,1)S(1)} %get-tuple-element.26.refs_0_.m1, bf16[32,1792]{1,0:T(8,128)(2,1)S(1)} %collective-permute-done.10.refs_1_, bf16[1792,1792]{1,0:T(8,128)(2,1)S(1)} %shard_map.61.refs_1_.refs_2_, bf16[1792,1792]{1,0:T(8,128)(2,1)S(1)} %get-tuple-element.18.refs_1_.refs_3_), custom_call_target="tpu_custom_call" | custom-call | tf_op jit(solution)/shard_map/pallas_call | solution.py:23
  43.6 1.2 %shard_map.67.before = f32[32,1792]{1,0:T(8,128)S(1)} custom-call(bf16[32,1792]{1,0:T(8,128)(2,1)S(1)} %collective-permute-done.8.block, bf16[1792,1792]{1,0:T(8,128)(2,1)S(1)} %get-tuple-element.20.refs_1_.tile, f32[32,1792]{1,0:T(8,128)S(1)} %shard_map.66.before), custom_call_target="tpu_custom_call" | custom-call | tf_op jit(solution)/shard_map/pallas_call | solution.py:23
  44.8 0.0 collective-permute-done.11.a1
  44.8 0.0 collective-permute-done.12.b1
  44.8 0.0 collective-permute-done.9.block
  44.8 1.4 %shard_map.68 = (bf16[32,1792]{1,0:T(8,128)(2,1)S(1)}, f32[16,128]{1,0:T(8,128)S(1)}) custom-call(bf16[32,1792]{1,0:T(8,128)(2,1)S(1)} %collective-permute-done.9.block, bf16[1792,1792]{1,0:T(8,128)(2,1)S(1)} %get-tuple-element.22.refs_1_.tile, f32[32,1792]{1,0:T(8,128)S(1)} %shard_map.67.before, f32[32,1792]{1,0:T(8,128)S(1)} %get-tuple-element.24.refs_3_.field_ref, ...), custom_call_target="tpu_custom_call" | custom-call | tf_op jit(solution)/shard_map/pallas_call | solution.py:23
  46.3 3.2 %collective-permute-start.13 = (bf16[32,1792]{1,0:T(8,128)(2,1)S(1)}, bf16[32,1792]{1,0:T(8,128)(2,1)S(1)}, u32[]{:S(2)}, u32[]{:S(2)}) collective-permute-start(bf16[32,1792]{1,0:T(8,128)(2,1)S(1)} %get-tuple-element.29.own), channel_id=1, source_target_pairs={{0,4},{8,12},{4,0},{12,8},{1,5},{9,13},{5,1},{13,9},{2,6},{10,14},... | collective-permute-start | bytes 344072 | tf_op jit(solution)/shard_map/ppermute | solution.py:175
  49.4 0.7 %collective-permute-start.14 = (bf16[32,1792]{1,0:T(8,128)(2,1)S(1)}, bf16[32,1792]{1,0:T(8,128)(2,1)S(1)}, u32[]{:S(2)}, u32[]{:S(2)}) collective-permute-start(bf16[32,1792]{1,0:T(8,128)(2,1)S(1)} %get-tuple-element.29.own), channel_id=1, source_target_pairs={{4,8},{8,4},{5,9},{9,5},{6,10},{10,6},{7,11},{11,7},{20,24},{24,20... | collective-permute-start | bytes 344072 | tf_op jit(solution)/shard_map/ppermute | solution.py:175
  50.1 11.6 %all_to_all.11 = f32[16,1,128]{2,1,0:T(1,128)S(1)} all-to-all(f32[16,1,128]{2,1,0:T(1,128)S(1)} %bitcast.5), channel_id=1, replica_groups=mesh['groups'=2,'tm'=4,'stn'=4] {'tm','stn'}, dimensions={0} | all-to-all | bytes 16384 | tf_op jit(solution)/shard_map/all_to_all | solution.py:319
  61.8 0.0 collective-permute-done.13.a
  61.8 0.0 collective-permute-done.14.b
  61.8 1.4 %shard_map.69 = (f32[32,1792]{1,0:T(8,128)}, f32[32,1792]{1,0:T(8,128)}) custom-call(f32[16,128]{1,0:T(8,128)S(1)} %bitcast.4, f32[32,1792]{1,0:T(8,128)S(1)} %get-tuple-element.24.refs_3_.field_ref, f32[32,1792]{1,0:T(8,128)S(1)} %get-tuple-element.27.image_ref, f32[32,1792]{1,0:T(8,128)S(1)} %get-tuple-element.25.refs_4_.gain_ref, ...), custom_call_target="tpu_custom_call" | custom-call | tf_op jit(solution)/shard_map/pallas_call | solution.py:23
Async XLA Ops:
  1.7 6.3 %collective-permute-start = (bf16[32,1792]{1,0:T(8,128)(2,1)S(1)}, bf16[32,1792]{1,0:T(8,128)(2,1)S(1)}, u32[]{:S(2)}, u32[]{:S(2)}) collective-permute-start(bf16[32,1792]{1,0:T(8,128)(2,1)S(1)} %get-tuple-element.16.own_ref.m0), channel_id=1, source_target_pairs={{0,4},{8,12},{4,0},{12,8},{1,5},{9,13},{5,1},{13,9},{2,6},{10,14},... | collective-permute-start | bytes 344072 | tf_op jit(solution)/shard_map/ppermute | solution.py:175
  4.8 3.1 %collective-permute-start.1 = (bf16[32,1792]{1,0:T(8,128)(2,1)S(1)}, bf16[32,1792]{1,0:T(8,128)(2,1)S(1)}, u32[]{:S(2)}, u32[]{:S(2)}) collective-permute-start(bf16[32,1792]{1,0:T(8,128)(2,1)S(1)} %get-tuple-element.16.own_ref.m0), channel_id=1, source_target_pairs={{4,8},{8,4},{5,9},{9,5},{6,10},{10,6},{7,11},{11,7},{20,24},{24,20... | collective-permute-start | bytes 344072 | tf_op jit(solution)/shard_map/ppermute | solution.py:175
  8.2 4.9 %collective-permute-start.2 = (bf16[32,1792]{1,0:T(8,128)(2,1)S(1)}, bf16[32,1792]{1,0:T(8,128)(2,1)S(1)}, u32[]{:S(2)}, u32[]{:S(2)}) collective-permute-start(bf16[32,1792]{1,0:T(8,128)(2,1)S(1)} %shard_map.60.refs_0_), channel_id=1, source_target_pairs={{2,0},{3,1},{0,2},{1,3},{6,4},{7,5},{4,6},{5,7},{10,8},{11,9},{8,1... | collective-permute-start | bytes 344072 | tf_op jit(solution)/shard_map/ppermute | solution.py:185
  9.9 14.9 %collective-permute-start.6 = (bf16[32,1792]{1,0:T(8,128)(2,1)S(1)}, bf16[32,1792]{1,0:T(8,128)(2,1)S(1)}, u32[]{:S(2)}, u32[]{:S(2)}) collective-permute-start(bf16[32,1792]{1,0:T(8,128)(2,1)S(1)} %shard_map.60.refs_0_), channel_id=1, source_target_pairs={{1,0},{0,1},{3,2},{2,3},{5,4},{4,5},{7,6},{6,7},{9,8},{8,9},{11,10... | collective-permute-start | bytes 344072 | tf_op jit(solution)/shard_map/ppermute | solution.py:185
  13.0 19.7 %collective-permute-start.3 = (bf16[32,1792]{1,0:T(8,128)(2,1)S(1)}, bf16[32,1792]{1,0:T(8,128)(2,1)S(1)}, u32[]{:S(2)}, u32[]{:S(2)}) collective-permute-start(bf16[32,1792]{1,0:T(8,128)(2,1)S(1)} %collective-permute-done.2.refs_0_), channel_id=1, source_target_pairs={{1,0},{0,1},{3,2},{2,3},{5,4},{4,5},{7,6},{6,7},{9,8},{8,9},{11,10... | collective-permute-start | bytes 344072 | tf_op jit(solution)/shard_map/ppermute | solution.py:197
  13.0 3.7 %collective-permute-start.4 = (s32[2,1792]{1,0:T(2,128)S(1)}, s32[2,1792]{1,0:T(2,128)S(1)}, u32[]{:S(2)}, u32[]{:S(2)}) collective-permute-start(s32[2,1792]{1,0:T(2,128)S(1)} %get-tuple-element.17.rows_ref.cols_ref), channel_id=1, source_target_pairs={{2,0},{3,1},{0,2},{1,3},{6,4},{7,5},{4,6},{5,7},{10,8},{11,9},{8,1... | collective-permute-start | bytes 43016 | tf_op jit(solution)/shard_map/ppermute | solution.py:185
  14.7 6.2 %collective-permute-start.7 = (s32[2,1792]{1,0:T(2,128)S(1)}, s32[2,1792]{1,0:T(2,128)S(1)}, u32[]{:S(2)}, u32[]{:S(2)}) collective-permute-start(s32[2,1792]{1,0:T(2,128)S(1)} %get-tuple-element.17.rows_ref.cols_ref), channel_id=1, source_target_pairs={{1,0},{0,1},{3,2},{2,3},{5,4},{4,5},{7,6},{6,7},{9,8},{8,9},{11,10... | collective-permute-start | bytes 43016 | tf_op jit(solution)/shard_map/ppermute | solution.py:185
  16.7 12.1 %collective-permute-start.5 = (s32[2,1792]{1,0:T(2,128)S(1)}, s32[2,1792]{1,0:T(2,128)S(1)}, u32[]{:S(2)}, u32[]{:S(2)}) collective-permute-start(s32[2,1792]{1,0:T(2,128)S(1)} %collective-permute-done.4.rows_ref), channel_id=1, source_target_pairs={{1,0},{0,1},{3,2},{2,3},{5,4},{4,5},{7,6},{6,7},{9,8},{8,9},{11,10... | collective-permute-start | bytes 43016 | tf_op jit(solution)/shard_map/ppermute | solution.py:197
  34.0 7.2 %collective-permute-start.8 = (bf16[32,1792]{1,0:T(8,128)(2,1)S(1)}, bf16[32,1792]{1,0:T(8,128)(2,1)S(1)}, u32[]{:S(2)}, u32[]{:S(2)}) collective-permute-start(bf16[32,1792]{1,0:T(8,128)(2,1)S(1)} %get-tuple-element.26.refs_0_.m1), channel_id=1, source_target_pairs={{2,0},{3,1},{0,2},{1,3},{6,4},{7,5},{4,6},{5,7},{10,8},{11,9},{8,1... | collective-permute-start | bytes 344072 | tf_op jit(solution)/shard_map/ppermute | solution.py:185
  35.7 5.6 %collective-permute-start.10 = (bf16[32,1792]{1,0:T(8,128)(2,1)S(1)}, bf16[32,1792]{1,0:T(8,128)(2,1)S(1)}, u32[]{:S(2)}, u32[]{:S(2)}) collective-permute-start(bf16[32,1792]{1,0:T(8,128)(2,1)S(1)} %get-tuple-element.26.refs_0_.m1), channel_id=1, source_target_pairs={{1,0},{0,1},{3,2},{2,3},{5,4},{4,5},{7,6},{6,7},{9,8},{8,9},{11,10... | collective-permute-start | bytes 344072 | tf_op jit(solution)/shard_map/ppermute | solution.py:185
  35.9 8.9 %collective-permute-start.11 = (bf16[32,1792]{1,0:T(8,128)(2,1)S(1)}, bf16[32,1792]{1,0:T(8,128)(2,1)S(1)}, u32[]{:S(2)}, u32[]{:S(2)}) collective-permute-start(bf16[32,1792]{1,0:T(8,128)(2,1)S(1)} %get-tuple-element.26.refs_0_.m1), channel_id=1, source_target_pairs={{0,4},{8,12},{4,0},{12,8},{1,5},{9,13},{5,1},{13,9},{2,6},{10,14},... | collective-permute-start | bytes 344072 | tf_op jit(solution)/shard_map/ppermute | solution.py:175
  40.5 4.3 %collective-permute-start.12 = (bf16[32,1792]{1,0:T(8,128)(2,1)S(1)}, bf16[32,1792]{1,0:T(8,128)(2,1)S(1)}, u32[]{:S(2)}, u32[]{:S(2)}) collective-permute-start(bf16[32,1792]{1,0:T(8,128)(2,1)S(1)} %get-tuple-element.26.refs_0_.m1), channel_id=1, source_target_pairs={{4,8},{8,4},{5,9},{9,5},{6,10},{10,6},{7,11},{11,7},{20,24},{24,20... | collective-permute-start | bytes 344072 | tf_op jit(solution)/shard_map/ppermute | solution.py:175
  41.2 3.6 %collective-permute-start.9 = (bf16[32,1792]{1,0:T(8,128)(2,1)S(1)}, bf16[32,1792]{1,0:T(8,128)(2,1)S(1)}, u32[]{:S(2)}, u32[]{:S(2)}) collective-permute-start(bf16[32,1792]{1,0:T(8,128)(2,1)S(1)} %collective-permute-done.8.block), channel_id=1, source_target_pairs={{1,0},{0,1},{3,2},{2,3},{5,4},{4,5},{7,6},{6,7},{9,8},{8,9},{11,10... | collective-permute-start | bytes 344072 | tf_op jit(solution)/shard_map/ppermute | solution.py:197
  46.3 15.5 %collective-permute-start.13 = (bf16[32,1792]{1,0:T(8,128)(2,1)S(1)}, bf16[32,1792]{1,0:T(8,128)(2,1)S(1)}, u32[]{:S(2)}, u32[]{:S(2)}) collective-permute-start(bf16[32,1792]{1,0:T(8,128)(2,1)S(1)} %get-tuple-element.29.own), channel_id=1, source_target_pairs={{0,4},{8,12},{4,0},{12,8},{1,5},{9,13},{5,1},{13,9},{2,6},{10,14},... | collective-permute-start | bytes 344072 | tf_op jit(solution)/shard_map/ppermute | solution.py:175
  49.4 12.3 %collective-permute-start.14 = (bf16[32,1792]{1,0:T(8,128)(2,1)S(1)}, bf16[32,1792]{1,0:T(8,128)(2,1)S(1)}, u32[]{:S(2)}, u32[]{:S(2)}) collective-permute-start(bf16[32,1792]{1,0:T(8,128)(2,1)S(1)} %get-tuple-element.29.own), channel_id=1, source_target_pairs={{4,8},{8,4},{5,9},{9,5},{6,10},{10,6},{7,11},{11,7},{20,24},{24,20... | collective-permute-start | bytes 344072 | tf_op jit(solution)/shard_map/ppermute | solution.py:175
